TPU v7x, 256 devices: a whole 4x4x8 slice. The times are simulated.
256 devices in a mesh: dp: 64 (over z, y, core), mp: 4 (over x).
Axes of the slice: x: 4, y: 4, z: 8, core: 2. Of those that a mesh axis runs over, the one named last changes fastest.
Arguments:
- prefix_hidden: bfloat16 [256, 1024, 2048], P(('dp', 'mp')), may hold values from -6 to 6
- prefix_len: int32 [256], P('dp'), may hold values from 256 to 1024
- actions: float32 [256, 50, 32], P('dp'), may hold values from -6 to 6
- noise: float32 [256, 50, 32], P('dp'), may hold values from -6 to 6
- time_index: int32 [256], P('dp'), may hold values from 0 to 999
- prefix_gain: float32 [2048], replicated, may hold values from 0.25 to 1.75
- key_weight: bfloat16 [2048, 256], P('dp'), may hold values from -0.125 to 0.125
- value_weight: bfloat16 [2048, 256], P('dp'), may hold values from -0.125 to 0.125
- action_in: bfloat16 [32, 1024], replicated, may hold values from -1 to 1
- attn_gain: float32 [1024], replicated, may hold values from 0.25 to 1.75
- query_w: bfloat16 [1024, 2048], P('dp', 'mp'), may hold values from -0.1875 to 0.1875
- akey_w: bfloat16 [1024, 256], P('dp'), may hold values from -0.1875 to 0.1875
- avalue_w: bfloat16 [1024, 256], P('dp'), may hold values from -0.1875 to 0.1875
- out_w: bfloat16 [2048, 1024], P('mp', 'dp'), may hold values from -0.125 to 0.125
- mlp_gain: float32 [1024], replicated, may hold values from 0.25 to 1.75
- gate_w: bfloat16 [1024, 4096], P('dp', 'mp'), may hold values from -0.1875 to 0.1875
- up_w: bfloat16 [1024, 4096], P('dp', 'mp'), may hold values from -0.1875 to 0.1875
- down_w: bfloat16 [4096, 1024], P('mp', 'dp'), may hold values from -0.09375 to 0.09375
- final_gain: float32 [1024], replicated, may hold values from 0.25 to 1.75
- head_w: bfloat16 [1024, 32], replicated, may hold values from -0.1875 to 0.1875
Outputs:
- velocity: float32 [256, 50, 32], P(('dp', 'mp'))
- ep_loss: float32 [256], P(('dp', 'mp'))
Inputs may be any that keep to these rules, and one draw needn't show every extreme that they name: `prefix_len`: prefix positions at or above an episode's length are padding that no output reads.
All inputs are finite; a program needn't handle non-finite values.
Results may differ from a plain program's by a relative error of at most 0.009.
Values may be sent and summed in bfloat16 or wider, within the bound.
A program may use at most 64 MiB of HBM per device.

v0:
```python
import math

import jax
import jax.numpy as jnp
from jax import lax
from jax.sharding import Mesh
from jax.sharding import PartitionSpec as P

TSTEPS = 1000
DP = ("dp_0", "dp_1", "dp_2")
DP_MP = ("dp_0", "dp_1", "dp_2", "mp")


def in_one_piece(arrays, axis, dim, along):
    ends, at = ([], 0)
    for a in arrays[:-1]:
        at += a.shape[along]
        ends.append(at)
    both = jnp.concatenate(arrays, axis=along)
    return tuple(jnp.split(lax.all_gather(both, axis, axis=dim, tiled=True), ends, axis=along))


def laid_out(parts, dim):
    parts = jnp.moveaxis(parts, 0, dim)
    lengths = parts.shape
    return parts.reshape(*lengths[:dim], lengths[dim] * lengths[dim + 1], *lengths[dim + 2 :])


def all_blocks(value, axes, order):
    parts = value
    for k in order:
        parts = lax.all_gather(parts, axes[k])
    done = order[::-1]
    back = [done.index(k) for k in range(len(axes))]
    parts = parts.transpose(*back, *range(len(axes), parts.ndim))
    return parts.reshape(-1, *value.shape)


def gather_axes(value, axes, order, dim):
    return laid_out(all_blocks(value, axes, order), dim)


def from_everyone(value, axis):
    size = lax.axis_size(axis)
    return lax.all_to_all(
        jnp.broadcast_to(value[None], (size, *value.shape)), axis, 0, 0, tiled=True
    )


def gathered_copies(value, axis, dim):
    return laid_out(from_everyone(value, axis), dim)


def in_blocks(value, dim, size):
    before, after = (value.shape[:dim], value.shape[dim + 1 :])
    return jnp.moveaxis(value.reshape(*before, size, -1, *after), dim, 0)


def sent_and_summed(value, axis, dim):
    parts = in_blocks(value, dim, lax.axis_size(axis))
    arrived = lax.all_to_all(parts, axis, split_axis=0, concat_axis=0, tiled=True)
    return arrived.astype(jnp.float32).sum(axis=0)


def rms(values, gain):
    return values * lax.rsqrt(jnp.mean(values * values, axis=-1, keepdims=True) + 1e-06) * gain


def time_embed(times, width):
    half = width // 2
    steps = jnp.arange(half, dtype=jnp.float32)
    period = 0.004 * jnp.power(jnp.float32(1000.0), steps / (half - 1))
    angle = times[:, None] * (2.0 * math.pi) / period[None, :]
    return jnp.concatenate([jnp.sin(angle), jnp.cos(angle)], axis=-1)


def attend(query, pkeys, pvals, akeys, avals, lengths):
    live = jnp.arange(pkeys.shape[1], dtype=jnp.int32)[None, :] < lengths[:, None]
    scores = jnp.einsum("erd,epd->erp", query, pkeys, preferred_element_type=jnp.float32)
    probs = jnp.where(live[:, None, :], jnp.exp(scores), 0.0)
    action_scores = jnp.einsum("erd,ecd->erc", query, akeys, preferred_element_type=jnp.float32)
    action_probs = jnp.exp(action_scores)
    denom = jnp.sum(probs, axis=-1) + jnp.sum(action_probs, axis=-1)
    weighted = jnp.einsum(
        "erp,epd->erd", probs.astype(jnp.bfloat16), pvals, preferred_element_type=jnp.float32
    )
    weighted = weighted + jnp.einsum(
        "erc,ecd->erd", action_probs.astype(jnp.bfloat16), avals, preferred_element_type=jnp.float32
    )
    return (weighted / denom[:, :, None]).astype(jnp.bfloat16)


def on_device(
    prefix_hidden,
    prefix_len,
    actions,
    noise,
    time_index,
    prefix_gain,
    key_weight,
    value_weight,
    action_in,
    attn_gain,
    query_w,
    akey_w,
    avalue_w,
    out_w,
    mlp_gain,
    gate_w,
    up_w,
    down_w,
    final_gain,
    head_w,
):
    own_eps, positions, width = prefix_hidden.shape
    group_eps, span, adim = actions.shape
    expert = action_in.shape[1]
    head_size = key_weight.shape[1]
    local_heads = query_w.shape[1] // head_size
    rows_total = group_eps * span
    own_rows = own_eps * span
    member = lax.axis_index("mp")
    first_row = member * own_rows
    first_ep = member * own_eps
    times = (time_index.astype(jnp.float32) + 0.5) / TSTEPS
    x_t = times[:, None, None] * noise + (1.0 - times)[:, None, None] * actions
    target = noise - actions
    x_in = x_t.reshape(rows_total, adim).astype(jnp.bfloat16)
    temb = time_embed(times, expert)
    h0 = (
        jnp.dot(x_in, action_in, preferred_element_type=jnp.float32).reshape(
            group_eps, span, expert
        )
        + temb[:, None, :]
    )
    h0 = h0.reshape(rows_total, expert)
    key_full, value_full = in_one_piece((key_weight, value_weight), DP, 0, 1)
    prefix_normed = rms(
        prefix_hidden.reshape(own_eps * positions, width).astype(jnp.float32), prefix_gain
    ).astype(jnp.bfloat16)
    pkeys = (
        jnp.dot(prefix_normed, key_full, preferred_element_type=jnp.float32)
        .astype(jnp.bfloat16)
        .reshape(own_eps, positions, head_size)
    )
    pvals = (
        jnp.dot(prefix_normed, value_full, preferred_element_type=jnp.float32)
        .astype(jnp.bfloat16)
        .reshape(own_eps, positions, head_size)
    )
    normed = rms(h0, attn_gain).astype(jnp.bfloat16)
    query_full, akey_full, avalue_full = in_one_piece((query_w, akey_w, avalue_w), DP, 0, 1)
    query = (
        jnp.dot(normed, query_full, preferred_element_type=jnp.float32) * head_size ** (-0.5)
    ).astype(jnp.bfloat16)
    akeys = (
        jnp.dot(normed, akey_full, preferred_element_type=jnp.float32)
        .astype(jnp.bfloat16)
        .reshape(group_eps, span, head_size)
    )
    avals = (
        jnp.dot(normed, avalue_full, preferred_element_type=jnp.float32)
        .astype(jnp.bfloat16)
        .reshape(group_eps, span, head_size)
    )
    own_akeys = lax.dynamic_slice_in_dim(akeys, first_ep, own_eps, 0)
    own_avals = lax.dynamic_slice_in_dim(avals, first_ep, own_eps, 0)
    own_lengths = lax.dynamic_slice_in_dim(prefix_len, first_ep, own_eps, 0)
    query_heads = query.reshape(group_eps, span, local_heads, head_size)
    arrived = lax.all_to_all(query_heads, "mp", split_axis=0, concat_axis=2, tiled=True)
    count = arrived.shape[1]
    all_heads = arrived.shape[2]
    flat = arrived.reshape(own_eps, count * all_heads, head_size)
    result = attend(flat, pkeys, pvals, own_akeys, own_avals, own_lengths)
    result = result.reshape(own_eps, count, all_heads, head_size)
    attn = lax.all_to_all(result, "mp", split_axis=2, concat_axis=0, tiled=True)
    attn = attn.reshape(rows_total, local_heads * head_size)
    out_full = gather_axes(out_w, DP, (1, 0, 2), 1)
    gate_full, up_full = in_one_piece((gate_w, up_w), DP, 0, 1)
    down_full = gathered_copies(down_w, DP, 1)
    h0_own = lax.dynamic_slice_in_dim(h0, first_row, own_rows, 0)
    h1 = h0_own + sent_and_summed(
        jnp.dot(attn, out_full, preferred_element_type=jnp.float32).astype(jnp.bfloat16), "mp", 0
    )
    mixed_own = rms(h1, mlp_gain).astype(jnp.bfloat16)
    mixed = gathered_copies(mixed_own, "mp", 0)
    gate = jnp.dot(mixed, gate_full, preferred_element_type=jnp.float32)
    upper = jnp.dot(mixed, up_full, preferred_element_type=jnp.float32)
    hidden = (jax.nn.gelu(gate, approximate=True) * upper).astype(jnp.bfloat16)
    h2 = h1 + sent_and_summed(
        jnp.dot(hidden, down_full, preferred_element_type=jnp.float32).astype(jnp.bfloat16), "mp", 0
    )
    final = rms(h2, final_gain).astype(jnp.bfloat16)
    velocity = jnp.dot(final, head_w, preferred_element_type=jnp.float32).reshape(
        own_eps, span, adim
    )
    own_target = lax.dynamic_slice_in_dim(target, first_ep, own_eps, 0)
    diff = velocity - own_target
    ep_loss = jnp.mean(diff * diff, axis=(1, 2))
    return (velocity, ep_loss)


def solution(mesh):
    split = Mesh(mesh.devices.reshape(8, 4, 2, mesh.shape["mp"]), ("dp_0", "dp_1", "dp_2", "mp"))
    placed = (
        P(DP_MP, None, None),
        P(DP),
        P(DP, None, None),
        P(DP, None, None),
        P(DP),
        P(),
        P(DP, None),
        P(DP, None),
        P(),
        P(),
        P(DP, "mp"),
        P(DP, None),
        P(DP, None),
        P("mp", DP),
        P(),
        P(DP, "mp"),
        P(DP, "mp"),
        P("mp", DP),
        P(),
        P(),
    )
    return jax.shard_map(
        on_device,
        mesh=split,
        in_specs=placed,
        out_specs=(P(DP_MP, None, None), P(DP_MP)),
        check_vma=False,
    )
```

profile of v0, /device:TPU:1, one launch (start us, length us, event | category | flops | bytes accessed | tf_op | source)
XLA Modules:
  0.0 307.1 jit_solution(8571584262315926728)
XLA Ops:
  7.3 1.4 pad_maximum_fusion.1
  8.7 1.4 pad_maximum_fusion.2
  10.2 10.6 %all-gather = bf16[2048,16]{0,1:T(8,128)(2,1)S(1)} all-gather(bf16[512,16]{0,1:T(8,128)(2,1)} %param.33), channel_id=2, replica_groups=mesh['dp_0'=8,'dp_1'=4,'dp_2'=2,'mp'=4] {'dp_1'}, dimensions={0}, use_global_device_ids=true | all-gather | bytes 81920 | tf_op jit(solution)/shard_map/all_gather | solution.py:32
  20.8 25.8 %all-gather.1 = bf16[32,512,16]{1,2,0:T(8,128)(2,1)} all-gather(bf16[4,512,16]{1,2,0:T(8,128)(2,1)S(1)} %bitcast.80), channel_id=3, replica_groups=mesh['dp_0'=8,'dp_1'=4,'dp_2'=2,'mp'=4] {'dp_0'}, dimensions={0}, use_global_device_ids=true | all-gather | bytes 589824 | tf_op jit(solution)/shard_map/all_gather | solution.py:32
  46.6 1.4 pad_maximum_fusion
  48.1 3.1 %fusion = f32[1024]{0:T(1024)S(1)} fusion(bf16[1,1024,2048]{2,1,0:T(8,128)(2,1)} %param.20), kind=kLoop, calls=%fused_computation.2 | loop fusion | flops 6290432 | bytes 4198400 | tf_op jit(solution)/shard_map/reduce_sum | solution.py:66
  52.6 0.6 iota_compare_fusion
  53.5 39.0 %all-gather.8.cloned.1.call-done = bf16[1024,1024]{1,0:T(8,128)(2,1)} async-done(((bf16[16,1024]{1,0:T(8,128)(2,1)}), bf16[1024,1024]{1,0:T(8,128)(2,1)}) %all-gather.8.cloned.1.call-update) | async-done | bytes 2097168 | tf_op jit(solution)/shard_map/all_gather | solution.py:20
  92.5 1.6 fusion.16
  94.1 0.7 reshape.174
  94.8 4.0 %all-to-all-start = ((bf16[4,50,2,256]{3,2,1,0:T(2,128)(2,1)}), bf16[4,50,2,256]{3,2,1,0:T(2,128)(2,1)S(1)}, u32[]{:S(2)}, u32[]{:S(2)}) async-start(bf16[4,50,2,256]{3,2,1,0:T(2,128)(2,1)} %reshape.174), calls=%async_computation | async-start | bytes 409600 | tf_op jit(solution)/shard_map/all_to_all | solution.py:170
  98.8 1.3 convolution_convert_fusion.5
  100.2 1.3 convolution_convert_fusion.4
  101.5 2.6 all-to-all-done
  104.6 65.6 %all-gather.10.cloned.1.call-done = bf16[2048,512]{1,0:T(8,128)(2,1)} async-done(((bf16[32,512]{1,0:T(8,128)(2,1)}), bf16[2048,512]{1,0:T(8,128)(2,1)}) %all-gather.10.cloned.1.call-update) | async-done | bytes 2097168 | tf_op jit(solution)/shard_map/all_gather | solution.py:20
  170.2 4.5 %fusion.62 = (f32[400]{0:T(512)S(1)}, bf16[400,1024]{1,0:T(8,128)(2,1)S(1)}) fusion(bf16[400,256]{1,0:T(8,128)(2,1)S(1)} %reshape.175, bf16[1,1024,2048]{2,1,0:T(8,128)(2,1)} %param.20, f32[2048]{0:T(1024)S(1)} %copy-done.9, f32[1024]{0:T(1024)S(1)} %add_rsqrt_fusion, bf16[2048,512]{1,0:T(8,128)(2,1)} %all-gather.10.cloned.1.call-done, ...), kind=kOutput, calls=%fused_computation.87 | convolution fusion | flops 1293336192 | bytes 6281792 | tf_op jit(solution)/shard_map/erd,epd->erp/dot_general | solution.py:79
  174.8 4.3 %fusion.20 = f32[400,256]{1,0:T(8,128)S(1)} fusion(bf16[1,1024,2048]{2,1,0:T(8,128)(2,1)} %param.20, f32[2048]{0:T(1024)S(1)} %copy-done.9, f32[1024]{0:T(1024)S(1)} %add_rsqrt_fusion, bf16[2048,512]{1,0:T(8,128)(2,1)} %all-gather.10.cloned.1.call-done, bf16[400,1024]{1,0:T(8,128)(2,1)S(1)} %get-tuple-element.14), kind=kOutput, calls=%fused_computation.24 | convolution fusion | flops 1292107776 | bytes 6483968 | tf_op jit(solution)/shard_map/erp,epd->erd/dot_general | solution.py:84
  179.4 0.7 copy.34
  180.1 4.0 %all-to-all-start.1 = ((bf16[1,50,8,256]{3,1,0,2:T(8,128)(2,1)}), bf16[1,50,8,256]{3,1,0,2:T(8,128)(2,1)S(1)}, u32[]{:S(2)}, u32[]{:S(2)}) async-start(bf16[1,50,8,256]{3,1,0,2:T(8,128)(2,1)} %copy.34), calls=%async_computation.1 | async-start | bytes 458752 | tf_op jit(solution)/shard_map/all_to_all | solution.py:176
  184.4 1.3 copy.38
  185.7 4.0 %all-to-all-done.1 = bf16[1,50,8,256]{3,1,0,2:T(8,128)(2,1)S(1)} async-done(((bf16[1,50,8,256]{3,1,0,2:T(8,128)(2,1)}), bf16[1,50,8,256]{3,1,0,2:T(8,128)(2,1)S(1)}, u32[]{:S(2)}, u32[]{:S(2)}) %all-to-all-start.1) | async-done | bytes 204832 | tf_op jit(solution)/shard_map/all_to_all | solution.py:176
  190.6 0.9 reshape.184
  191.4 3.5 %all-to-all-start.2 = ((bf16[4,50,1024]{2,1,0:T(8,128)(2,1)}), bf16[4,50,1024]{2,1,0:T(8,128)(2,1)S(1)}, u32[]{:S(2)}, u32[]{:S(2)}) async-start(bf16[4,50,1024]{2,1,0:T(8,128)(2,1)} %reshape.184), calls=%async_computation.2 | async-start | bytes 917504 | tf_op jit(solution)/shard_map/all_to_all | solution.py:61
  194.9 6.8 %all-to-all-done.2 = bf16[4,50,1024]{2,1,0:T(8,128)(2,1)S(1)} async-done(((bf16[4,50,1024]{2,1,0:T(8,128)(2,1)}), bf16[4,50,1024]{2,1,0:T(8,128)(2,1)S(1)}, u32[]{:S(2)}, u32[]{:S(2)}) %all-to-all-start.2) | async-done | bytes 409632 | tf_op jit(solution)/shard_map/all_to_all | solution.py:61
  202.1 9.0 %all_to_all.50 = bf16[4,50,1024]{2,1,0:T(8,128)(2,1)S(1)} all-to-all(bf16[4,50,1024]{2,1,0:T(8,128)(2,1)S(1)} %broadcast_in_dim.14), channel_id=1, replica_groups=mesh['dp_0'=8,'dp_1'=4,'dp_2'=2,'mp'=4] {'mp'}, dimensions={0} | all-to-all | bytes 819200 | tf_op jit(solution)/shard_map/all_to_all | solution.py:45
  211.1 1.6 broadcast_in_dim.15
  212.7 10.4 %all-to-all-start.4 = ((bf16[64,1024,16]{1,2,0:T(8,128)(2,1)}), bf16[64,1024,16]{1,2,0:T(8,128)(2,1)S(1)}, u32[]{:S(2)}, u32[]{:S(2)}) async-start(bf16[64,1024,16]{1,2,0:T(8,128)(2,1)} %broadcast_in_dim.15), calls=%async_computation.4 | async-start | bytes 4194304 | tf_op jit(solution)/shard_map/all_to_all | solution.py:45
  223.2 56.3 %all-gather.12.cloned.1.call-done = bf16[1024,2048]{1,0:T(8,128)(2,1)} async-done(((bf16[16,2048]{1,0:T(8,128)(2,1)}), bf16[1024,2048]{1,0:T(8,128)(2,1)}) %all-gather.12.cloned.1.call-update) | async-done | bytes 4194320 | tf_op jit(solution)/shard_map/all_gather | solution.py:20
  279.6 3.3 %fusion.37 = f32[200,1024]{1,0:T(8,128)} fusion(bf16[200,1024]{1,0:T(8,128)(2,1)S(1)} %reshape.185, bf16[1024,2048]{1,0:T(8,128)(2,1)} %all-gather.12.cloned.1.call-done), kind=kOutput, calls=%fused_computation.41 | convolution fusion | flops 421068800 | bytes 3325952 | tf_op jit(solution)/shard_map/dot_general | solution.py:187
  282.8 3.1 convolution_convert_fusion.2
  286.0 11.1 %all_to_all.51 = bf16[4,50,1024]{2,1,0:T(8,128)(2,1)S(1)} all-to-all(bf16[4,50,1024]{2,1,0:T(8,128)(2,1)S(1)} %reshape.187), channel_id=1, replica_groups=mesh['dp_0'=8,'dp_1'=4,'dp_2'=2,'mp'=4] {'mp'}, dimensions={0} | all-to-all | bytes 819200 | tf_op jit(solution)/shard_map/all_to_all | solution.py:61
  297.3 1.4 fusion.55
  (65 shorter events, 4.5 us)
Async XLA Ops:
  7.2 44.2 %copy-start = (bf16[32,1024]{1,0:T(8,128)(2,1)S(1)}, bf16[32,1024]{1,0:T(8,128)(2,1)}, u32[]{:S(2)}) copy-start(bf16[32,1024]{1,0:T(8,128)(2,1)} %param.28) | copy-start | bytes 196612
  7.2 44.0 %copy-start.8 = (s32[4]{0:T(128)S(1)}, s32[4]{0:T(128)}, u32[]{:S(2)}) copy-start(s32[4]{0:T(128)} %param.24) | copy-start | bytes 52
  7.2 44.2 %copy-start.1 = (f32[4,50,32]{1,2,0:T(8,128)S(1)}, f32[4,50,32]{1,2,0:T(8,128)}, u32[]{:S(2)}) copy-start(f32[4,50,32]{1,2,0:T(8,128)} %param.22) | copy-start | bytes 76804
  7.2 44.2 %copy-start.2 = (f32[4,50,32]{1,2,0:T(8,128)S(1)}, f32[4,50,32]{1,2,0:T(8,128)}, u32[]{:S(2)}) copy-start(f32[4,50,32]{1,2,0:T(8,128)} %param.23) | copy-start | bytes 76804
  7.2 85.2 %all-gather.8.cloned.1.call-start = ((), (), s32[]{:S(2)}) async-start(), calls=%async_computation.6 | async-start | bytes 2129920 | tf_op jit(solution)/shard_map/all_gather | solution.py:20
  8.7 161.5 %all-gather.10.cloned.1.call-start = ((), (), s32[]{:S(2)}) async-start(), calls=%async_computation.7 | async-start | bytes 2129920 | tf_op jit(solution)/shard_map/all_gather | solution.py:20
  10.1 174.3 %all-gather.14.cloned.1.call-start = ((), (), s32[]{:S(2)}) async-start(), calls=%async_computation.9 | async-start | bytes 1572864 | tf_op jit(solution)/shard_map/all_gather | solution.py:32
  20.8 31.3 %copy-start.10 = (s32[4]{0:T(128)S(1)}, s32[4]{0:T(128)}, u32[]{:S(2)}) copy-start(s32[4]{0:T(128)} %param.21) | copy-start | bytes 52
  20.8 32.5 %copy-start.5 = (f32[1024]{0:T(1024)S(1)}, f32[1024]{0:T(1024)}, u32[]{:S(2)}) copy-start(f32[1024]{0:T(1024)} %param.29) | copy-start | bytes 12292
  46.6 233.0 %all-gather.12.cloned.1.call-start = ((), (), s32[]{:S(2)}) async-start(), calls=%async_computation.8 | async-start | bytes 4259840 | tf_op jit(solution)/shard_map/all_gather | solution.py:20
  51.9 118.3 %copy-start.9 = (f32[2048]{0:T(1024)S(1)}, f32[2048]{0:T(1024)}, u32[]{:S(2)}) copy-start(f32[2048]{0:T(1024)} %param.25) | copy-start | bytes 24580
  94.8 9.3 %all-to-all-start = ((bf16[4,50,2,256]{3,2,1,0:T(2,128)(2,1)}), bf16[4,50,2,256]{3,2,1,0:T(2,128)(2,1)S(1)}, u32[]{:S(2)}, u32[]{:S(2)}) async-start(bf16[4,50,2,256]{3,2,1,0:T(2,128)(2,1)} %reshape.174), calls=%async_computation | async-start | bytes 409600 | tf_op jit(solution)/shard_map/all_to_all | solution.py:170
  180.1 9.6 %all-to-all-start.1 = ((bf16[1,50,8,256]{3,1,0,2:T(8,128)(2,1)}), bf16[1,50,8,256]{3,1,0,2:T(8,128)(2,1)S(1)}, u32[]{:S(2)}, u32[]{:S(2)}) async-start(bf16[1,50,8,256]{3,1,0,2:T(8,128)(2,1)} %copy.34), calls=%async_computation.1 | async-start | bytes 458752 | tf_op jit(solution)/shard_map/all_to_all | solution.py:176
  184.1 17.9 %copy-start.6 = (f32[1024]{0:T(1024)S(1)}, f32[1024]{0:T(1024)}, u32[]{:S(2)}) copy-start(f32[1024]{0:T(1024)} %param.34) | copy-start | bytes 12292
  185.7 25.4 %copy-start.4 = (bf16[1024,16]{0,1:T(8,128)(2,1)S(1)}, bf16[1024,16]{0,1:T(8,128)(2,1)}, u32[]{:S(2)}) copy-start(bf16[1024,16]{0,1:T(8,128)(2,1)} %param.37) | copy-start | bytes 98308
  191.4 10.3 %all-to-all-start.2 = ((bf16[4,50,1024]{2,1,0:T(8,128)(2,1)}), bf16[4,50,1024]{2,1,0:T(8,128)(2,1)S(1)}, u32[]{:S(2)}, u32[]{:S(2)}) async-start(bf16[4,50,1024]{2,1,0:T(8,128)(2,1)} %reshape.184), calls=%async_computation.2 | async-start | bytes 917504 | tf_op jit(solution)/shard_map/all_to_all | solution.py:61
  212.7 70.1 %all-to-all-start.4 = ((bf16[64,1024,16]{1,2,0:T(8,128)(2,1)}), bf16[64,1024,16]{1,2,0:T(8,128)(2,1)S(1)}, u32[]{:S(2)}, u32[]{:S(2)}) async-start(bf16[64,1024,16]{1,2,0:T(8,128)(2,1)} %broadcast_in_dim.15), calls=%async_computation.4 | async-start | bytes 4194304 | tf_op jit(solution)/shard_map/all_to_all | solution.py:45
  282.8 14.5 %copy-start.3 = (bf16[1024,32]{0,1:T(8,128)(2,1)S(1)}, bf16[1024,32]{0,1:T(8,128)(2,1)}, u32[]{:S(2)}) copy-start(bf16[1024,32]{0,1:T(8,128)(2,1)} %param.39) | copy-start | bytes 196612
  282.8 14.5 %copy-start.7 = (f32[1024]{0:T(1024)S(1)}, f32[1024]{0:T(1024)}, u32[]{:S(2)}) copy-start(f32[1024]{0:T(1024)} %param.38) | copy-start | bytes 12292
Sparse Core Ops, SparseCore 0:
  10.8 81.5 all-gather.7
  95.2 74.9 all-gather.9
  172.0 12.3 all-gather.13
  187.0 92.5 all-gather.11
where the time goes:
time: 309 us; the launch traced here: 307 us
  waiting for transfers between devices  175 us (57%)
  blocking collectives  56.4 us (18%)
  matrix products  22.3 us (7%)
  starting transfers between devices  22 us (7%)
  between operations  15.9 us (5%)
  other arithmetic  8.73 us (3%)
  local copies, waits for them, and re-layouts  7.03 us (2%)
    all_gather x3, waiting for transfers between devices, in_one_piece(): lax.all_gather(both, axis, axis=dim, tiled=True)  161 us
    all_gather x2, blocking collectives, all_blocks(): parts = lax.all_gather(parts, axes[k])  36.4 us
    all_to_all x1, blocking collectives, sent_and_summed(): lax.all_to_all(parts, axis, split_axis=0, concat_axis=0, tiled=True)  11.1 us
    all_to_all x1, starting transfers between devices, from_everyone(): lax.all_to_all(jnp.broadcast_to(value[None], (size, *value.shape)), axis,...  10.4 us
    all_to_all x1, blocking collectives, from_everyone(): lax.all_to_all(jnp.broadcast_to(value[None], (size, *value.shape)), axis,...  8.96 us
    all_to_all x1, waiting for transfers between devices, sent_and_summed(): lax.all_to_all(parts, axis, split_axis=0, concat_axis=0, tiled=True)  6.83 us
  transfers between devices with their start and end apart: 8, of which 7 were waited for; matrix products, arithmetic and copies ran while one was open for 10% of the time, Pallas kernels for 0%

commit v1 on v0

v1 whole, which is shorter than its diff:
```python
import functools
import math

import jax
import jax.numpy as jnp
from jax import lax
from jax.experimental import pallas as pl
from jax.experimental.pallas import tpu as pltpu
from jax.sharding import Mesh
from jax.sharding import PartitionSpec as P

TSTEPS = 1000
NZ, NY, NC, NX = 8, 4, 2, 4
DP_MP = ("z", "y", "c", "mp")
DP = ("z", "y", "c")
MESH = pl.DeviceIdType.MESH


class Gather:
    def __init__(self, buf, order, send_sem, recv_sem, where):
        self.buf, self.order = buf, order
        self.ss, self.rs = send_sem, recv_sem
        self.z, self.y, self.c = where
        self.n = 0
        self.sent = []
        self.waiting = []
        self.steps = self.plan()

    def at(self, dim, ring_index, part=None):
        size = NZ if dim == "z" else NY
        ring_index = lax.rem(ring_index + size, size)
        first = dim == self.order[0]
        cols = self.buf.shape[-1]
        if dim == "z":
            if first:
                if part is None:
                    return self.buf.at[ring_index, self.y, self.c]
                return self.buf.at[ring_index, self.y, self.c, :, pl.ds(part * cols // 2, cols // 2)]
            if part is None:
                return self.buf.at[ring_index, :, self.c]
            return self.buf.at[ring_index, pl.ds(part * (NY // 2), NY // 2), self.c]
        if first:
            if part is None:
                return self.buf.at[self.z, ring_index, self.c]
            return self.buf.at[self.z, ring_index, self.c, :, pl.ds(part * cols // 2, cols // 2)]
        if part is None:
            return self.buf.at[:, ring_index, self.c]
        return self.buf.at[pl.ds(part * (NZ // 2), NZ // 2), ring_index, self.c]

    def send(self, view, device):
        k = self.n
        self.n += 1
        copy = pltpu.make_async_remote_copy(
            src_ref=view,
            dst_ref=view,
            send_sem=self.ss.at[k],
            recv_sem=self.rs.at[k],
            device_id=device,
            device_id_type=MESH,
        )
        copy.start()
        self.sent.append(copy)
        self.waiting.append(copy)

    def arrive(self):
        for copy in self.waiting:
            copy.wait_recv()
        self.waiting = []

    def ring_step(self, dim, hop):
        size, me = (NZ, self.z) if dim == "z" else (NY, self.y)
        up = {dim: lax.rem(me + 1, size)}
        down = {dim: lax.rem(me + size - 1, size)}
        self.arrive()
        if hop < size // 2:
            self.send(self.at(dim, me - hop + 1), up)
            self.send(self.at(dim, me + hop - 1), down)
        else:
            self.send(self.at(dim, me - hop + 1, 0), up)
            self.send(self.at(dim, me + hop - 1, 1), down)

    def core_step(self):
        self.arrive()
        self.send(self.buf.at[:, :, self.c], {"c": 1 - self.c})

    def plan(self):
        steps = []
        for dim in self.order:
            for hop in range(1, (NZ if dim == "z" else NY) // 2 + 1):
                steps.append(functools.partial(self.ring_step, dim, hop))
        steps.append(self.core_step)
        steps.append(self.arrive)
        return steps

    def finish(self):
        for copy in self.sent:
            copy.wait_send()


SENDS = 13
ORDERS = ("zy", "yz", "zy", "yz", "yz", "zy", "yz", "zy")
STARTS = (0, 0, 1, 1, 2, 3, 3, 4)


def gather_kernel(*refs):
    n = len(ORDERS)
    blocks, bufs = refs[:n], refs[n : 2 * n]
    send_sem, recv_sem = refs[2 * n :]
    z, y, c = (lax.axis_index(a) for a in ("z", "y", "c"))
    barrier = pltpu.get_barrier_semaphore()
    near = (
        {"z": lax.rem(z + 1, NZ)},
        {"z": lax.rem(z + NZ - 1, NZ)},
        {"y": lax.rem(y + 1, NY)},
        {"y": lax.rem(y + NY - 1, NY)},
        {"c": 1 - c},
    )
    for device in near:
        pl.semaphore_signal(barrier, inc=1, device_id=device, device_id_type=MESH)
    for block, buf in zip(blocks, bufs):
        buf[z, y, c] = block[...]
    pl.semaphore_wait(barrier, len(near))
    gathers = [
        Gather(buf, order, send_sem.at[i], recv_sem.at[i], (z, y, c))
        for i, (buf, order) in enumerate(zip(bufs, ORDERS))
    ]
    last = max(s + len(g.steps) for s, g in zip(STARTS, gathers))
    for tick in range(last):
        for start, g in zip(STARTS, gathers):
            if 0 <= tick - start < len(g.steps):
                g.steps[tick - start]()
    for g in gathers:
        g.finish()


def gather_all(*blocks):
    n = len(blocks)
    vmem = pl.BlockSpec(memory_space=pltpu.VMEM)
    return pl.pallas_call(
        gather_kernel,
        out_shape=[jax.ShapeDtypeStruct((NZ, NY, NC, *b.shape), b.dtype) for b in blocks],
        in_specs=[vmem] * n,
        out_specs=[vmem] * n,
        scratch_shapes=[
            pltpu.SemaphoreType.DMA((n, SENDS)),
            pltpu.SemaphoreType.DMA((n, SENDS)),
        ],
        compiler_params=pltpu.CompilerParams(
            collective_id=0, has_side_effects=True, vmem_limit_bytes=40 << 20
        ),
    )(*blocks)


def from_everyone(value, axis):
    size = lax.axis_size(axis)
    return lax.all_to_all(
        jnp.broadcast_to(value[None], (size, *value.shape)), axis, 0, 0, tiled=True
    )


def sent_and_summed(value, axis):
    size = lax.axis_size(axis)
    parts = value.reshape(size, -1, *value.shape[1:])
    arrived = lax.all_to_all(parts, axis, split_axis=0, concat_axis=0, tiled=True)
    return arrived.astype(jnp.float32).sum(axis=0)


def rms(values, gain):
    return values * lax.rsqrt(jnp.mean(values * values, axis=-1, keepdims=True) + 1e-06) * gain


def time_embed(times, width):
    half = width // 2
    steps = jnp.arange(half, dtype=jnp.float32)
    period = 0.004 * jnp.power(jnp.float32(1000.0), steps / (half - 1))
    angle = times[:, None] * (2.0 * math.pi) / period[None, :]
    return jnp.concatenate([jnp.sin(angle), jnp.cos(angle)], axis=-1)


def attend(query, pkeys, pvals, akeys, avals, lengths):
    live = jnp.arange(pkeys.shape[1], dtype=jnp.int32)[None, :] < lengths[:, None]
    scores = jnp.einsum("erd,epd->erp", query, pkeys, preferred_element_type=jnp.float32)
    probs = jnp.where(live[:, None, :], jnp.exp(scores), 0.0)
    action_scores = jnp.einsum("erd,ecd->erc", query, akeys, preferred_element_type=jnp.float32)
    action_probs = jnp.exp(action_scores)
    denom = jnp.sum(probs, axis=-1) + jnp.sum(action_probs, axis=-1)
    weighted = jnp.einsum(
        "erp,epd->erd", probs.astype(jnp.bfloat16), pvals, preferred_element_type=jnp.float32
    )
    weighted = weighted + jnp.einsum(
        "erc,ecd->erd", action_probs.astype(jnp.bfloat16), avals, preferred_element_type=jnp.float32
    )
    return (weighted / denom[:, :, None]).astype(jnp.bfloat16)


def on_device(
    prefix_hidden,
    prefix_len,
    actions,
    noise,
    time_index,
    prefix_gain,
    key_weight,
    value_weight,
    action_in,
    attn_gain,
    query_w,
    akey_w,
    avalue_w,
    out_w,
    mlp_gain,
    gate_w,
    up_w,
    down_w,
    final_gain,
    head_w,
):
    f32, bf16 = jnp.float32, jnp.bfloat16
    own_eps, positions, width = prefix_hidden.shape
    group_eps, span, adim = actions.shape
    expert = action_in.shape[1]
    head_size = key_weight.shape[1]
    local_heads = query_w.shape[1] // head_size
    rows_total = group_eps * span
    own_rows = own_eps * span
    member = lax.axis_index("mp")
    first_row = member * own_rows
    first_ep = member * own_eps
    blocks = (
        key_weight,
        value_weight,
        query_w,
        jnp.concatenate([akey_w, avalue_w], axis=1),
        out_w.T,
        gate_w,
        up_w,
        down_w.T,
    )
    full = [w.reshape(-1, w.shape[-1]) for w in gather_all(*blocks)]
    key_full, value_full, query_full, action_kv, out_t, gate_full, up_full, down_t = full
    times = (time_index.astype(f32) + 0.5) / TSTEPS
    x_t = times[:, None, None] * noise + (1.0 - times)[:, None, None] * actions
    target = noise - actions
    x_in = x_t.reshape(rows_total, adim).astype(bf16)
    temb = time_embed(times, expert)
    h0 = (
        jnp.dot(x_in, action_in, preferred_element_type=f32).reshape(group_eps, span, expert)
        + temb[:, None, :]
    )
    h0 = h0.reshape(rows_total, expert)
    prefix_normed = rms(
        prefix_hidden.reshape(own_eps * positions, width).astype(f32), prefix_gain
    ).astype(bf16)
    pkeys = (
        jnp.dot(prefix_normed, key_full, preferred_element_type=f32)
        .astype(bf16)
        .reshape(own_eps, positions, head_size)
    )
    pvals = (
        jnp.dot(prefix_normed, value_full, preferred_element_type=f32)
        .astype(bf16)
        .reshape(own_eps, positions, head_size)
    )
    normed = rms(h0, attn_gain).astype(bf16)
    query = (
        jnp.dot(normed, query_full, preferred_element_type=f32) * head_size ** (-0.5)
    ).astype(bf16)
    both = jnp.dot(normed, action_kv, preferred_element_type=f32).astype(bf16)
    akeys = both[:, :head_size].reshape(group_eps, span, head_size)
    avals = both[:, head_size:].reshape(group_eps, span, head_size)
    own_akeys = lax.dynamic_slice_in_dim(akeys, first_ep, own_eps, 0)
    own_avals = lax.dynamic_slice_in_dim(avals, first_ep, own_eps, 0)
    own_lengths = lax.dynamic_slice_in_dim(prefix_len, first_ep, own_eps, 0)
    query_heads = query.reshape(group_eps, span, local_heads, head_size)
    arrived = lax.all_to_all(query_heads, "mp", split_axis=0, concat_axis=2, tiled=True)
    count = arrived.shape[1]
    all_heads = arrived.shape[2]
    flat = arrived.reshape(own_eps, count * all_heads, head_size)
    result = attend(flat, pkeys, pvals, own_akeys, own_avals, own_lengths)
    result = result.reshape(own_eps, count, all_heads, head_size)
    attn = lax.all_to_all(result, "mp", split_axis=2, concat_axis=0, tiled=True)
    attn = attn.reshape(rows_total, local_heads * head_size)
    h0_own = lax.dynamic_slice_in_dim(h0, first_row, own_rows, 0)
    h1 = h0_own + sent_and_summed(
        jnp.einsum("rk,nk->rn", attn, out_t, preferred_element_type=f32).astype(bf16), "mp"
    )
    mixed_own = rms(h1, mlp_gain).astype(bf16)
    mixed = from_everyone(mixed_own, "mp").reshape(rows_total, expert)
    gate = jnp.dot(mixed, gate_full, preferred_element_type=f32)
    upper = jnp.dot(mixed, up_full, preferred_element_type=f32)
    hidden = (jax.nn.gelu(gate, approximate=True) * upper).astype(bf16)
    h2 = h1 + sent_and_summed(
        jnp.einsum("rk,nk->rn", hidden, down_t, preferred_element_type=f32).astype(bf16), "mp"
    )
    final = rms(h2, final_gain).astype(bf16)
    velocity = jnp.dot(final, head_w, preferred_element_type=f32).reshape(own_eps, span, adim)
    own_target = lax.dynamic_slice_in_dim(target, first_ep, own_eps, 0)
    diff = velocity - own_target
    ep_loss = jnp.mean(diff * diff, axis=(1, 2))
    return (velocity, ep_loss)


def solution(mesh):
    split = Mesh(mesh.devices.reshape(NZ, NY, NC, NX), DP_MP)
    placed = (
        P(DP_MP, None, None),
        P(DP),
        P(DP, None, None),
        P(DP, None, None),
        P(DP),
        P(),
        P(DP, None),
        P(DP, None),
        P(),
        P(),
        P(DP, "mp"),
        P(DP, None),
        P(DP, None),
        P("mp", DP),
        P(),
        P(DP, "mp"),
        P(DP, "mp"),
        P("mp", DP),
        P(),
        P(),
    )
    return jax.shard_map(
        on_device,
        mesh=split,
        in_specs=placed,
        out_specs=(P(DP_MP, None, None), P(DP_MP)),
        check_vma=False,
    )
```

time: 309 us -> 170 us (0.55)
  the two profiles are of different devices: /device:TPU:1 before, /device:TPU:2 now
where the time goes in v1:
time: 170 us; the launch traced here: 169 us
  Pallas kernels  68 us (40%)
  blocking collectives  29.9 us (18%)
  matrix products  24.8 us (15%)
  local copies, waits for them, and re-layouts  21.6 us (13%)
  starting transfers between devices  9.85 us (6%)
  other arithmetic  6.83 us (4%)
  waiting for transfers between devices  5.07 us (3%)
  between operations  2.67 us (2%)
    pallas_call x1, Pallas kernels, gather_all(): pl.pallas_call(gather_kernel, out_shape=[jax.ShapeDtypeStruct((NZ, NY, NC...  68 us
    unnamed x43, local copies, waits for them, and re-layouts  10.8 us
    all_to_all x1, blocking collectives, from_everyone(): lax.all_to_all(jnp.broadcast_to(value[None], (size, *value.shape)), axis,...  10.1 us
    all_to_all x1, blocking collectives, sent_and_summed(): lax.all_to_all(parts, axis, split_axis=0, concat_axis=0, tiled=True)  10.1 us
    all_to_all x1, blocking collectives, on_device(): attn = lax.all_to_all(result, 'mp', split_axis=2, concat_axis=0, tiled=True)  9.64 us
    dot_general x1, matrix products, attend(): jnp.einsum('erp,epd->erd', probs.astype(jnp.bfloat16), pvals, preferred_e...  5.36 us
    dot_general x1, matrix products, attend(): jnp.einsum('erd,epd->erp', query, pkeys, preferred_element_type=jnp.float32)  5.34 us
    all_to_all x1, waiting for transfers between devices, sent_and_summed(): lax.all_to_all(parts, axis, split_axis=0, concat_axis=0, tiled=True)  5.07 us
  transfers between devices with their start and end apart: 2, of which 1 were waited for; matrix products, arithmetic and copies ran while one was open for 5% of the time, Pallas kernels for 0%

profile of v1, /device:TPU:2, one launch (start us, length us, event | category | flops | bytes accessed | tf_op | source)
XLA Modules:
  0.0 168.7 jit_solution(17036356859753236433)
XLA Ops:
  1.5 1.3 multiply_reduce_fusion
  2.9 0.9 multiply_convert_fusion
  3.8 0.9 convert_element_type.75
  5.4 0.8 copy-done.3
  6.2 0.8 copy-done.4
  10.5 68.0 %shard_map.203 = (bf16[8,4,2,32,256]{4,3,2,1,0:T(8,128)(2,1)S(1)}, bf16[8,4,2,32,256]{4,3,2,1,0:T(8,128)(2,1)S(1)}, bf16[8,4,2,16,512]{4,3,2,1,0:T(8,128)(2,1)S(...) custom-call(bf16[32,256]{1,0:T(8,128)(2,1)S(1)} %copy-done.6, ...), custom_call_target="tpu_custom_call" | custom-call | tf_op jit(solution)/shard_map/pallas_call | solution.py:139
  78.6 1.0 copy-done.1
  79.5 1.3 copy-done.10
  80.8 1.3 copy-done.11
  82.2 1.0 copy-done.12
  83.2 1.0 copy-done.13
  84.2 1.4 fusion.8
  86.3 5.0 %all-to-all-start = ((bf16[4,50,2,256]{3,2,1,0:T(2,128)(2,1)}), bf16[4,50,2,256]{3,2,1,0:T(2,128)(2,1)S(1)}, u32[]{:S(2)}, u32[]{:S(2)}) async-start(bf16[4,50,2,256]{3,2,1,0:T(2,128)(2,1)} %reshape.231), calls=%async_computation | async-start | bytes 409600 | tf_op jit(solution)/shard_map/all_to_all | solution.py:275
  91.3 3.2 %fusion = f32[1024]{0:T(1024)S(1)} fusion(bf16[1,1024,2048]{2,1,0:T(8,128)(2,1)} %param.20), kind=kLoop, calls=%fused_computation.2 | loop fusion | flops 6290432 | bytes 4198400 | tf_op jit(solution)/shard_map/reduce_sum | solution.py:169
  95.5 1.6 reshape.238
  99.0 0.8 copy.25
  99.8 1.0 reshape.232
  100.9 1.0 fusion.56
  101.8 5.3 %fusion.53 = (f32[400]{0:T(512)S(1)}, bf16[400,1024]{1,0:T(8,128)(2,1)}) fusion(bf16[400,256]{1,0:T(8,128)(2,1)S(1)} %reshape.232, bf16[2048,256]{1,0:T(8,128)(2,1)} %bitcast.77, bf16[1,1024,2048]{2,1,0:T(8,128)(2,1)} %param.20, f32[2048]{0:T(1024)S(1)} %copy-done.19, f32[1024]{0:T(1024)S(1)} %add_rsqrt_fusion, pred[1024]{0:T(1024)(128)(4,1)S(1)} %iota_compare_fusion), kind=kOutput, calls=%fused_computation.84 | convolution fusion | flops 1293336192 | bytes 6281792 | tf_op jit(solution)/shard_map/erd,epd->erp/dot_general | solution.py:182
  107.2 5.4 %fusion.12 = f32[400,256]{1,0:T(8,128)} fusion(bf16[2048,256]{1,0:T(8,128)(2,1)} %bitcast.76, bf16[1,1024,2048]{2,1,0:T(8,128)(2,1)} %param.20, f32[2048]{0:T(1024)S(1)} %copy-done.19, f32[1024]{0:T(1024)S(1)} %add_rsqrt_fusion, bf16[400,1024]{1,0:T(8,128)(2,1)} %get-tuple-element.32), kind=kOutput, calls=%fused_computation.22 | convolution fusion | flops 1292107776 | bytes 6483968 | tf_op jit(solution)/shard_map/erp,epd->erd/dot_general | solution.py:187
  112.5 1.3 fusion.10
  113.9 9.6 %all_to_all.45 = bf16[1,50,8,256]{3,1,0,2:T(8,128)(2,1)S(1)} all-to-all(bf16[1,50,8,256]{3,1,0,2:T(8,128)(2,1)S(1)} %copy.26), channel_id=1, replica_groups=mesh['z'=8,'y'=4,'c'=2,'mp'=4] {'mp'}, dimensions={2} | all-to-all | bytes 409600 | tf_op jit(solution)/shard_map/all_to_all | solution.py:281
  123.9 1.3 convolution_convert_fusion.3
  125.1 1.9 %reshape.243 = bf16[4,50,1024]{2,1,0:T(8,128)(2,1)} reshape(bf16[200,1024]{1,0:T(8,128)(2,1)} %convolution_convert_fusion.3) | data formatting | bytes 819200 | tf_op jit(solution)/shard_map/reshape | solution.py:163
  127.1 4.9 %all-to-all-start.2 = ((bf16[4,50,1024]{2,1,0:T(8,128)(2,1)}), bf16[4,50,1024]{2,1,0:T(8,128)(2,1)S(1)}, u32[]{:S(2)}, u32[]{:S(2)}) async-start(bf16[4,50,1024]{2,1,0:T(8,128)(2,1)} %reshape.243), calls=%async_computation.2 | async-start | bytes 917504 | tf_op jit(solution)/shard_map/all_to_all | solution.py:164
  131.9 1.3 reshape.229
  133.2 5.1 %all-to-all-done.2 = bf16[4,50,1024]{2,1,0:T(8,128)(2,1)S(1)} async-done(((bf16[4,50,1024]{2,1,0:T(8,128)(2,1)}), bf16[4,50,1024]{2,1,0:T(8,128)(2,1)S(1)}, u32[]{:S(2)}, u32[]{:S(2)}) %all-to-all-start.2) | async-done | bytes 409632 | tf_op jit(solution)/shard_map/all_to_all | solution.py:164
  138.7 10.1 %all_to_all.46 = bf16[4,50,1024]{2,1,0:T(8,128)(2,1)S(1)} all-to-all(bf16[4,50,1024]{2,1,0:T(8,128)(2,1)S(1)} %broadcast_in_dim.12), channel_id=1, replica_groups=mesh['z'=8,'y'=4,'c'=2,'mp'=4] {'mp'}, dimensions={0} | all-to-all | bytes 819200 | tf_op jit(solution)/shard_map/all_to_all | solution.py:156
  148.9 1.5 fusion.57
  150.4 3.8 %convolution_convert_fusion.2 = bf16[200,1024]{1,0:T(8,128)(2,1)S(1)} fusion(bf16[1024,1024]{1,0:T(8,128)(2,1)} %bitcast.75, bf16[200,1024]{1,0:T(8,128)(2,1)S(1)} %reshape.244, bf16[1024,1024]{1,0:T(8,128)(2,1)} %bitcast.74, f32[200,1024]{1,0:T(8,128)} %fusion.57), kind=kOutput, calls=%fused_computation.12 | convolution fusion | flops 841113600 | bytes 5832704 | tf_op jit(solution)/shard_map/rk,nk->rn/dot_general | solution.py:293
  154.4 10.1 %all_to_all.47 = bf16[4,50,1024]{2,1,0:T(8,128)(2,1)S(1)} all-to-all(bf16[4,50,1024]{2,1,0:T(8,128)(2,1)S(1)} %reshape.248), channel_id=1, replica_groups=mesh['z'=8,'y'=4,'c'=2,'mp'=4] {'mp'}, dimensions={0} | all-to-all | bytes 819200 | tf_op jit(solution)/shard_map/all_to_all | solution.py:164
  164.7 2.2 %fusion.41 = (f32[]{:T(128)}, f32[1,50,32]{1,2,0:T(8,128)}) fusion(f32[4,50,32]{1,2,0:T(8,128)} %param.22, s32[]{:T(128)S(6)} %select_n.15, f32[4,50,32]{1,2,0:T(8,128)} %param.23, bf16[1024,32]{0,1:T(8,128)(2,1)S(1)} %copy-done.16, f32[50,1024]{1,0:T(8,128)S(1)} %get-tuple-element.19, f32[1024]{0:T(1024)S(1)} %copy-done.18, f32[50]{0:T(128)S(1)} %add_rsqrt_fusion.2), kind=kOutput, calls=%fused_computation.61 | convolution fusion | flops 3436799 | bytes 293840 | tf_op jit(solution)/shard_map/dot_general | solution.py:296
  (64 shorter events, 10.1 us)
Async XLA Ops:
  0.6 0.9 copy-start
  2.8 2.6 %copy-start.14 = (f32[4,50,1024]{2,1,0:T(8,128)}, f32[4,50,1024]{2,1,0:T(8,128)S(1)}, u32[]{:S(2)}) copy-start(f32[4,50,1024]{2,1,0:T(8,128)S(1)} %get-tuple-element.30) | copy-start | bytes 2457604
  5.4 0.8 copy-start.3
  6.2 0.8 copy-start.4
  6.9 0.8 copy-start.5
  7.7 0.7 copy-start.6
  8.4 0.7 copy-start.7
  9.1 0.7 copy-start.8
  9.8 0.7 copy-start.9
  78.5 1.0 copy-start.1
  79.5 1.3 copy-start.10
  80.8 1.3 copy-start.11
  82.2 1.0 copy-start.12
  83.2 1.0 copy-start.13
  84.2 13.6 %copy-start.20 = (s32[4]{0:T(128)S(1)}, s32[4]{0:T(128)}, u32[]{:S(2)}) copy-start(s32[4]{0:T(128)} %param.21) | copy-start | bytes 52
  86.3 15.5 %copy-start.19 = (f32[2048]{0:T(1024)S(1)}, f32[2048]{0:T(1024)}, u32[]{:S(2)}) copy-start(f32[2048]{0:T(1024)} %param.25) | copy-start | bytes 24580
  86.3 12.7 %all-to-all-start = ((bf16[4,50,2,256]{3,2,1,0:T(2,128)(2,1)}), bf16[4,50,2,256]{3,2,1,0:T(2,128)(2,1)S(1)}, u32[]{:S(2)}, u32[]{:S(2)}) async-start(bf16[4,50,2,256]{3,2,1,0:T(2,128)(2,1)} %reshape.231), calls=%async_computation | async-start | bytes 409600 | tf_op jit(solution)/shard_map/all_to_all | solution.py:275
  91.3 3.2 %copy-start.2 = (bf16[8,4,2,16,512]{4,3,2,1,0:T(8,128)(2,1)S(1)}, bf16[8,4,2,16,512]{4,3,2,1,0:T(8,128)(2,1)}, u32[]{:S(2)}) copy-start(bf16[8,4,2,16,512]{4,3,2,1,0:T(8,128)(2,1)} %copy-done.1) | copy-start | bytes 3145732
  91.3 3.2 %copy-start.15 = (bf16[200,1024]{1,0:T(8,128)(2,1)S(1)}, bf16[200,1024]{1,0:T(8,128)(2,1)}, u32[]{:S(2)}) copy-start(bf16[200,1024]{1,0:T(8,128)(2,1)} %convert_element_type.75) | copy-start | bytes 1228804
  113.9 24.7 %copy-start.17 = (f32[1024]{0:T(1024)S(1)}, f32[1024]{0:T(1024)}, u32[]{:S(2)}) copy-start(f32[1024]{0:T(1024)} %param.34) | copy-start | bytes 12292
  127.1 11.2 %all-to-all-start.2 = ((bf16[4,50,1024]{2,1,0:T(8,128)(2,1)}), bf16[4,50,1024]{2,1,0:T(8,128)(2,1)S(1)}, u32[]{:S(2)}, u32[]{:S(2)}) async-start(bf16[4,50,1024]{2,1,0:T(8,128)(2,1)} %reshape.243), calls=%async_computation.2 | async-start | bytes 917504 | tf_op jit(solution)/shard_map/all_to_all | solution.py:164
  150.4 14.3 %copy-start.16 = (bf16[1024,32]{0,1:T(8,128)(2,1)S(1)}, bf16[1024,32]{0,1:T(8,128)(2,1)}, u32[]{:S(2)}) copy-start(bf16[1024,32]{0,1:T(8,128)(2,1)} %param.39) | copy-start | bytes 196612
  150.4 14.3 %copy-start.18 = (f32[1024]{0:T(1024)S(1)}, f32[1024]{0:T(1024)}, u32[]{:S(2)}) copy-start(f32[1024]{0:T(1024)} %param.38) | copy-start | bytes 12292

commit v2 on v0

v2 whole, which is shorter than its diff:
```python
import functools
import math

import jax
import jax.numpy as jnp
import numpy as np
from jax import lax
from jax.experimental import pallas as pl
from jax.experimental.pallas import tpu as pltpu
from jax.sharding import Mesh
from jax.sharding import PartitionSpec as P

TSTEPS = 1000
NZ, NY, NC, NX = 8, 4, 2, 4
SIZE = {"z": NZ, "y": NY, "c": NC, "mp": NX}
DP_MP = ("z", "y", "c", "mp")
DP = ("z", "y", "c")
MESH = pl.DeviceIdType.MESH
PAD = 64
SENDS = 160
LOCALS = 32
f32, bf16 = jnp.float32, jnp.bfloat16


def nt(a, b):
    return lax.dot_general(a, b, (((1,), (1,)), ((), ())), preferred_element_type=f32)


def dot(a, b):
    return jnp.dot(a, b, preferred_element_type=f32)


class Link:
    def __init__(self, send_sem, recv_sem):
        self.ss, self.rs = send_sem, recv_sem
        self.me = {a: lax.axis_index(a) for a in SIZE}
        self.sent = []

    def peer(self, axis, step):
        return {axis: lax.rem(self.me[axis] + step + SIZE[axis], SIZE[axis])}

    def send(self, src, dst, axis, step):
        k = len(self.sent)
        copy = pltpu.make_async_remote_copy(
            src_ref=src,
            dst_ref=dst,
            send_sem=self.ss.at[k],
            recv_sem=self.rs.at[k],
            device_id=self.peer(axis, step),
            device_id_type=MESH,
        )
        copy.start()
        self.sent.append(copy)
        return copy


class Gather:
    def __init__(self, link, buf, plan):
        self.link, self.buf = link, buf
        self.waiting = []
        self.steps = []
        for first, (dim, form) in zip((True, False), plan):
            if form == "ring":
                for hop in range(1, SIZE[dim] // 2 + 1):
                    self.steps.append(functools.partial(self.ring, dim, first, hop))
            elif form == "direct":
                self.steps.append(functools.partial(self.direct, dim, first))
            else:
                self.steps.append(functools.partial(self.two, dim, first, 1))
                self.steps.append(functools.partial(self.two, dim, first, 2))
        self.steps.append(self.core)
        self.steps.append(self.arrive)

    def at(self, dim, first, step, part=None):
        me = self.link.me
        i = lax.rem(me[dim] + step + SIZE[dim], SIZE[dim])
        cols = self.buf.shape[-1]
        half = pl.ds(0 if part is None else part * (cols // 2), cols // 2)
        if dim == "z":
            if first:
                if part is None:
                    return self.buf.at[i, me["y"], me["c"]]
                return self.buf.at[i, me["y"], me["c"], :, half]
            if part is None:
                return self.buf.at[i, :, me["c"]]
            return self.buf.at[i, pl.ds(part * (NY // 2), NY // 2), me["c"]]
        if first:
            if part is None:
                return self.buf.at[me["z"], i, me["c"]]
            return self.buf.at[me["z"], i, me["c"], :, half]
        if part is None:
            return self.buf.at[:, i, me["c"]]
        return self.buf.at[pl.ds(part * (NZ // 2), NZ // 2), i, me["c"]]

    def send(self, view, axis, step):
        self.waiting.append(self.link.send(view, view, axis, step))

    def arrive(self):
        for copy in self.waiting:
            copy.wait_recv()
        self.waiting = []

    def ring(self, dim, first, hop):
        self.arrive()
        last = hop == SIZE[dim] // 2
        self.send(self.at(dim, first, 1 - hop, 0 if last else None), dim, 1)
        self.send(self.at(dim, first, hop - 1, 1 if last else None), dim, -1)

    def direct(self, dim, first):
        self.arrive()
        for step in range(1, SIZE[dim]):
            self.send(self.at(dim, first, 0), dim, step)

    def two(self, dim, first, hop):
        self.arrive()
        if hop == 1:
            for step in (1, -1, 2, -2):
                self.send(self.at(dim, first, 0), dim, step)
        else:
            self.send(self.at(dim, first, -2), dim, 1)
            self.send(self.at(dim, first, 2), dim, -1)
            self.send(self.at(dim, first, -2, 0), dim, 2)
            self.send(self.at(dim, first, 2, 1), dim, -2)

    def core(self):
        self.arrive()
        self.send(self.buf.at[:, :, self.link.me["c"]], "c", 1)

    def step(self):
        if self.steps:
            self.steps.pop(0)()

    def finish(self):
        while self.steps:
            self.step()


def flat(ref):
    return ref[...].reshape(-1, ref.shape[-1])


def norm_rows(src, dst, gain, rows, block=16, unroll=4):
    start, count = rows

    def body(i, _):
        at = pl.ds(pl.multiple_of(start + i * block, block), block)
        v = src[at, :].astype(f32)
        scale = lax.rsqrt(jnp.mean(v * v, axis=-1, keepdims=True) + 1e-06)
        dst[at, :] = (v * scale * gain[...]).astype(bf16)
        return 0

    lax.fori_loop(0, count // block, body, 0, unroll=unroll)


def kernel(
    lens,
    tix,
    x_in,
    acts,
    noise,
    prefix,
    inv_period,
    prefix_gain,
    attn_gain,
    mlp_gain,
    final_gain,
    action_in,
    head_t,
    key_w,
    value_w,
    query_w,
    akey_w,
    avalue_w,
    out_t,
    gate_w,
    up_w,
    down_t,
    vel_ref,
    loss_ref,
    kb,
    vb,
    qb,
    ab,
    ob,
    gb,
    ub,
    db,
    pre,
    pk,
    pv,
    ain,
    hdt,
    actv,
    noisev,
    h0,
    an,
    akv,
    qs,
    qall,
    ares,
    aall,
    part,
    r1,
    r2,
    h1,
    mn,
    hid,
    fn,
    send_sem,
    recv_sem,
    local_sem,
):
    link = Link(send_sem, recv_sem)
    me = link.me
    z, y, c, x = (me[a] for a in DP_MP)
    span = 50

    locals_ = []

    def fetch(src, dst):
        copy = pltpu.make_async_copy(src, dst, local_sem.at[len(locals_)])
        copy.start()
        locals_.append(copy)
        return copy

    barrier = pltpu.get_barrier_semaphore()
    near = [("z", s) for s in (1, -1, 2, -2)] + [("y", s) for s in (1, 2, 3)]
    near += [("c", 1)] + [("mp", s) for s in (1, 2, 3)]
    for axis, step in near:
        pl.semaphore_signal(barrier, inc=1, device_id=link.peer(axis, step), device_id_type=MESH)
    early = [
        fetch(key_w, kb.at[z, y, c]),
        fetch(query_w, qb.at[z, y, c]),
        fetch(value_w, vb.at[z, y, c]),
        fetch(akey_w, ab.at[z, y, c, :, pl.ds(0, 256)]),
        fetch(avalue_w, ab.at[z, y, c, :, pl.ds(256, 256)]),
    ]
    small = [
        fetch(action_in, ain),
        fetch(head_t, hdt),
        fetch(acts, actv),
        fetch(noise, noisev),
    ]
    quarter = prefix.shape[0] // 4
    chunks = [
        fetch(prefix.at[pl.ds(i * quarter, quarter)], pre.at[pl.ds(i * quarter, quarter)])
        for i in range(4)
    ]
    late = [
        fetch(out_t, ob.at[z, y, c]),
        fetch(gate_w, gb.at[z, y, c]),
        fetch(up_w, ub.at[z, y, c]),
        fetch(down_t, db.at[z, y, c]),
    ]
    keys = Gather(link, kb, (("z", "two"), ("y", "direct")))
    query = Gather(link, qb, (("z", "two"), ("y", "direct")))
    values = Gather(link, vb, (("y", "direct"), ("z", "two")))
    action = Gather(link, ab, (("z", "two"), ("y", "direct")))
    out = Gather(link, ob, (("y", "ring"), ("z", "ring")))
    gate = Gather(link, gb, (("z", "two"), ("y", "ring")))
    up = Gather(link, ub, (("y", "ring"), ("z", "ring")))
    down = Gather(link, db, (("z", "two"), ("y", "ring")))

    def advance(*gathers):
        for g in gathers:
            g.step()

    for copy in early:
        copy.wait()
    pl.semaphore_wait(barrier, len(near))
    advance(query, keys, values, action)

    for copy in small:
        copy.wait()
    for e in range(4):
        t = (tix[e].astype(f32) + 0.5) * (1.0 / TSTEPS)
        u = t * inv_period[...]
        turn = (u - jnp.floor(u + 0.5)) * (2.0 * math.pi)
        half = turn.shape[1]
        at = pl.ds(e * PAD, PAD)
        mixed = dot(x_in[at, :], ain[...])
        h0[at, 0:half] = mixed[:, 0:half] + jnp.sin(turn)
        h0[at, half:] = mixed[:, half:] + jnp.cos(turn)
    norm_rows(h0, an, attn_gain, (0, 4 * PAD))
    advance(query, keys, values, action)
    for copy in late:
        copy.wait()
    chunks[0].wait()
    norm_rows(pre, pre, prefix_gain, (0, quarter))
    advance(query, keys, values, action)
    advance(gate, out, up)
    chunks[1].wait()
    norm_rows(pre, pre, prefix_gain, (quarter, quarter))
    advance(query, keys, action, values)
    advance(down, out, up, gate)
    chunks[2].wait()
    norm_rows(pre, pre, prefix_gain, (2 * quarter, quarter))
    query.finish()
    q = (dot(an[...], flat(qb)) * 0.0625).astype(bf16)
    for e in range(4):
        for h in range(2):
            qs[e, h] = q[e * PAD : (e + 1) * PAD, h * 256 : (h + 1) * 256]
    queries = [None]
    for step in range(1, NX):
        queries.append(link.send(qs.at[lax.rem(x + step, NX)], qall.at[x], "mp", step))
    qall[x] = qs[x]
    advance(down, out, up, gate)
    chunks[3].wait()
    norm_rows(pre, pre, prefix_gain, (3 * quarter, quarter))
    keys.finish()
    full_key = flat(kb)
    for i in range(4):
        at = pl.ds(i * quarter, quarter)
        pk[at, :] = dot(pre[at, :], full_key).astype(bf16)
    action.finish()
    own = pl.ds(pl.multiple_of(x * PAD, PAD), PAD)
    akv[...] = dot(an[own, :], flat(ab)).astype(bf16)
    advance(down, out, up, gate)
    values.finish()
    full_value = flat(vb)
    for i in range(4):
        at = pl.ds(i * quarter, quarter)
        pv[at, :] = dot(pre[at, :], full_value).astype(bf16)
    advance(down, out, up, gate)

    length = lens[x]
    heads = []
    for step in (0, 1, 2, 3):
        src = lax.rem(x - step + NX, NX)
        if step:
            queries[step].wait_recv()
        rows = qall[src].reshape(2 * PAD, 256)
        s = nt(rows, pk[...])
        live = lax.broadcasted_iota(jnp.int32, s.shape, 1) < length
        p = jnp.where(live, jnp.exp(s), 0.0)
        sa = nt(rows, akv[:, 0:256])
        real = lax.broadcasted_iota(jnp.int32, sa.shape, 1) < span
        pa = jnp.where(real, jnp.exp(sa), 0.0)
        total = jnp.sum(p, axis=-1, keepdims=True) + jnp.sum(pa, axis=-1, keepdims=True)
        mixed = dot(p.astype(bf16), pv[...]) + dot(pa.astype(bf16), akv[:, 256:512])
        done = (mixed / total).astype(bf16).reshape(2, PAD, 256)
        if step:
            ares[step] = done
            heads.append(link.send(ares.at[step], aall.at[x], "mp", -step))
        else:
            aall[x] = done
        advance(down, out, up, gate)

    def exchange(src, dst):
        return [
            link.send(src.at[lax.rem(x + step, NX)], dst.at[step], "mp", step)
            for step in range(1, NX)
        ]

    out.finish()
    for copy in heads:
        copy.wait_recv()
    a0 = aall[:, 0].reshape(4 * PAD, 256)
    a1 = aall[:, 1].reshape(4 * PAD, 256)
    full_out = flat(ob)
    for j in range(4):
        w = full_out[j * 256 : (j + 1) * 256]
        value = (nt(a0, w[:, 0:256]) + nt(a1, w[:, 256:512])).astype(bf16)
        part[:, :, j * 256 : (j + 1) * 256] = value.reshape(4, PAD, 256)
    sums = exchange(part, r1)
    advance(down, up, gate)
    own_h0 = h0[own, :] + part[x].astype(f32)
    for copy in sums:
        copy.wait_recv()
    h1[...] = own_h0 + r1[1].astype(f32) + r1[2].astype(f32) + r1[3].astype(f32)
    norm_rows(h1, mn.at[x], mlp_gain, (0, PAD))
    rows_sent = [link.send(mn.at[x], mn.at[x], "mp", step) for step in range(1, NX)]
    gate.finish()
    up.finish()
    for copy in rows_sent:
        copy.wait_recv()
    full_mn = mn[...].reshape(4 * PAD, -1)
    for j in range(4):
        cols = pl.ds(j * 256, 256)
        wg = gb[:, :, :, :, cols].reshape(-1, 256)
        wu = ub[:, :, :, :, cols].reshape(-1, 256)
        act = jax.nn.gelu(dot(full_mn, wg), approximate=True)
        hid[:, cols] = (act * dot(full_mn, wu)).astype(bf16)
    down.finish()
    for copy in sums:
        copy.wait_send()
    full_down = flat(db)
    for j in range(4):
        value = nt(hid[...], full_down[j * 256 : (j + 1) * 256]).astype(bf16)
        part[:, :, j * 256 : (j + 1) * 256] = value.reshape(4, PAD, 256)
    sums2 = exchange(part, r2)
    own_h1 = h1[...] + part[x].astype(f32)
    for copy in sums2:
        copy.wait_recv()
    h1[...] = own_h1 + r2[1].astype(f32) + r2[2].astype(f32) + r2[3].astype(f32)
    norm_rows(h1, fn, final_gain, (0, PAD))
    velocity = nt(hdt[...], fn[...])[:, 0:span]
    vel_ref[0] = velocity
    diff = velocity - (noisev[x] - actv[x])
    square = jnp.sum(diff * diff, axis=0, keepdims=True)
    loss_ref[...] = jnp.sum(square, axis=1, keepdims=True) / (span * 32.0)
    waited = {id(copy) for copy in sums}
    for copy in link.sent:
        if id(copy) not in waited:
            copy.wait_send()


def on_device(
    prefix_hidden,
    prefix_len,
    actions,
    noise,
    time_index,
    prefix_gain,
    key_weight,
    value_weight,
    action_in,
    attn_gain,
    query_w,
    akey_w,
    avalue_w,
    out_w,
    mlp_gain,
    gate_w,
    up_w,
    down_w,
    final_gain,
    head_w,
):
    positions, width = prefix_hidden.shape[1:]
    group_eps, span, adim = actions.shape
    expert = action_in.shape[1]
    times = (time_index.astype(f32) + 0.5) / TSTEPS
    x_t = times[:, None, None] * noise + (1.0 - times)[:, None, None] * actions
    x_in = jnp.pad(x_t.astype(bf16), ((0, 0), (0, PAD - span), (0, 0)))
    x_in = x_in.reshape(group_eps * PAD, adim)
    half = expert // 2
    inv_period = (250.0 * 1000.0 ** (-np.arange(half) / (half - 1))).astype(np.float32)
    vmem = pl.BlockSpec(memory_space=pltpu.VMEM)
    smem = pl.BlockSpec(memory_space=pltpu.SMEM)
    hbm = pl.BlockSpec(memory_space=pltpu.HBM)
    operands = [
        (prefix_len, smem),
        (time_index, smem),
        (x_in, vmem),
        (actions.transpose(0, 2, 1), hbm),
        (noise.transpose(0, 2, 1), hbm),
        (prefix_hidden.reshape(positions, width), hbm),
        (jnp.asarray(inv_period)[None, :], vmem),
        (prefix_gain[None, :], vmem),
        (attn_gain[None, :], vmem),
        (mlp_gain[None, :], vmem),
        (final_gain[None, :], vmem),
        (action_in, hbm),
        (head_w.T, hbm),
        (key_weight, hbm),
        (value_weight, hbm),
        (query_w, hbm),
        (akey_w, hbm),
        (avalue_w, hbm),
        (out_w.T, hbm),
        (gate_w, hbm),
        (up_w, hbm),
        (down_w.T, hbm),
    ]

    def weight(rows, cols):
        return pltpu.VMEM((NZ, NY, NC, rows, cols), bf16)

    rows = group_eps * PAD
    velocity, loss = pl.pallas_call(
        kernel,
        out_shape=(
            jax.ShapeDtypeStruct((1, adim, span), f32),
            jax.ShapeDtypeStruct((1, 1), f32),
        ),
        in_specs=[spec for _, spec in operands],
        out_specs=(vmem, vmem),
        scratch_shapes=[
            weight(32, 256),
            weight(32, 256),
            weight(16, 512),
            weight(16, 512),
            weight(16, 512),
            weight(16, 1024),
            weight(16, 1024),
            weight(16, 1024),
            pltpu.VMEM((positions, width), bf16),
            pltpu.VMEM((positions, 256), bf16),
            pltpu.VMEM((positions, 256), bf16),
            pltpu.VMEM((adim, expert), bf16),
            pltpu.VMEM((adim, expert), bf16),
            pltpu.VMEM((group_eps, adim, span), f32),
            pltpu.VMEM((group_eps, adim, span), f32),
            pltpu.VMEM((rows, expert), f32),
            pltpu.VMEM((rows, expert), bf16),
            pltpu.VMEM((PAD, 512), bf16),
            pltpu.VMEM((NX, 2, PAD, 256), bf16),
            pltpu.VMEM((NX, 2, PAD, 256), bf16),
            pltpu.VMEM((NX, 2, PAD, 256), bf16),
            pltpu.VMEM((NX, 2, PAD, 256), bf16),
            pltpu.VMEM((NX, PAD, expert), bf16),
            pltpu.VMEM((NX, PAD, expert), bf16),
            pltpu.VMEM((NX, PAD, expert), bf16),
            pltpu.VMEM((PAD, expert), f32),
            pltpu.VMEM((NX, PAD, expert), bf16),
            pltpu.VMEM((rows, 1024), bf16),
            pltpu.VMEM((PAD, expert), bf16),
            pltpu.SemaphoreType.DMA((SENDS,)),
            pltpu.SemaphoreType.DMA((SENDS,)),
            pltpu.SemaphoreType.DMA((LOCALS,)),
        ],
        compiler_params=pltpu.CompilerParams(
            collective_id=0, has_side_effects=True, vmem_limit_bytes=56 << 20
        ),
    )(*[value for value, _ in operands])
    return velocity.transpose(0, 2, 1), loss.reshape(1)


def solution(mesh):
    split = Mesh(mesh.devices.reshape(NZ, NY, NC, NX), DP_MP)
    placed = (
        P(DP_MP, None, None),
        P(DP),
        P(DP, None, None),
        P(DP, None, None),
        P(DP),
        P(),
        P(DP, None),
        P(DP, None),
        P(),
        P(),
        P(DP, "mp"),
        P(DP, None),
        P(DP, None),
        P("mp", DP),
        P(),
        P(DP, "mp"),
        P(DP, "mp"),
        P("mp", DP),
        P(),
        P(),
    )
    return jax.shard_map(
        on_device,
        mesh=split,
        in_specs=placed,
        out_specs=(P(DP_MP, None, None), P(DP_MP)),
        check_vma=False,
    )
```

time: 309 us -> 107 us (0.35)
  waiting for transfers between devices: 175 us -> 0 us
  Pallas kernels: 0 us -> 100 us
  blocking collectives: 56.4 us -> 0 us
  matrix products: 22.3 us -> 0 us
  starting transfers between devices: 22 us -> 0 us
  between operations: 15.9 us -> 2.46 us
  other arithmetic: 8.73 us -> 1.61 us
  local copies, waits for them, and re-layouts: 7.03 us -> 2.08 us
    all_gather x4 -> x0, waiting for transfers between devices: 161 us -> none  [the longest x3 161 us: in_one_piece(): lax.all_gather(both, axis, axis=dim, tiled=True)]
    pallas_call x0 -> x1, Pallas kernels: none -> 100 us  [on_device(): pl.pallas_call(kernel, out_shape=(jax.ShapeDtypeStruct((1, adim, span), f...]
    all_gather x2 -> x0, blocking collectives: 36.4 us -> none  [all_blocks(): parts = lax.all_gather(parts, axes[k])]
    dot_general x12 -> x0, matrix products: 22.3 us -> none  [the longest x1 4.53 us: attend(): jnp.einsum('erd,epd->erp', query, pkeys, preferred_element_type=jnp.float32)]
    all_to_all x4 -> x0, starting transfers between devices: 21.8 us -> none  [the longest x1 10.4 us: from_everyone(): lax.all_to_all(jnp.broadcast_to(value[None], (size, *value.shape)), axis,...]
    all_to_all x2 -> x0, blocking collectives: 20 us -> none  [the longest x1 11.1 us: sent_and_summed(): lax.all_to_all(parts, axis, split_axis=0, concat_axis=0, tiled=True)]
    all_to_all x4 -> x0, waiting for transfers between devices: 13.4 us -> none  [the longest x1 6.83 us: sent_and_summed(): lax.all_to_all(parts, axis, split_axis=0, concat_axis=0, tiled=True)]
    concatenate x4 -> x0, other arithmetic: 4.15 us -> none  [the longest x3 4.15 us: in_one_piece(): both = jnp.concatenate(arrays, axis=along)]
  transfers between devices with their start and end apart: 8 -> 0, of which waited for: 7 -> 0; matrix products, arithmetic and copies ran while one was open for 10% -> 0% of each run, Pallas kernels for 0% -> 0%
where the time goes in v2:
time: 107 us
  Pallas kernels  100 us (93%)
  between operations  2.46 us (2%)
  local copies, waits for them, and re-layouts  2.08 us (2%)
  other arithmetic  1.61 us (2%)
    pallas_call x1, Pallas kernels, on_device(): pl.pallas_call(kernel, out_shape=(jax.ShapeDtypeStruct((1, adim, span), f...  100 us

profile of v2, /device:TPU:1, one launch (start us, length us, event | category | flops | bytes accessed | tf_op | source)
XLA Modules:
  0.0 106.5 jit_solution(15953155810595473025)
XLA Ops:
  0.6 0.7 add_multiply_fusion
  1.3 1.0 add_convert_fusion
  2.2 0.1 copy.24
  2.4 0.6 pad.4.clone
  3.0 100.4 %shard_map.212 = (f32[1,32,50]{2,1,0:T(8,128)}, f32[1,1]{1,0:T(1,128)}) custom-call(s32[4]{0:T(128)} %lens.1, s32[4]{0:T(128)} %tix.1, bf16[256,32]{1,0:T(8,128)(2,1)} %bitcast.16, f32[4,32,50]{2,1,0:T(8,128)} %bitcast.14, f32[4,32,50]{2,1,0:T(8,128)} %bitcast.15, bf16[1024,2048]{1,0:T(8,128)(2,1)} %bitcast.13, f32[1,512]{1,0:T(1,128)} %constant.29.inv_period, ...), custom_call_target="tpu_custom_call" | custom-call | tf_op jit(solution)/shard_map/pallas_call | solution.py:471
  103.4 1.3 %copy.27 = f32[1,50,32]{1,2,0:T(8,128)} copy(f32[1,50,32]{1,2,0:T(8,128)} %bitcast.20) | data formatting | bytes 12800

commit v3 on v2

v3 whole, which is shorter than its diff:
```python
import functools
import math

import jax
import jax.numpy as jnp
import numpy as np
from jax import lax
from jax.experimental import pallas as pl
from jax.experimental.pallas import tpu as pltpu
from jax.sharding import Mesh
from jax.sharding import PartitionSpec as P

TSTEPS = 1000
NZ, NY, NC, NX = 8, 4, 2, 4
SIZE = {"z": NZ, "y": NY, "c": NC, "mp": NX}
DP_MP = ("z", "y", "c", "mp")
DP = ("z", "y", "c")
MESH = pl.DeviceIdType.MESH
PAD = 64
ROWS = 56
SENDS = 192
LOCALS = 32
f32, bf16 = jnp.float32, jnp.bfloat16


def nt(a, b):
    return lax.dot_general(a, b, (((1,), (1,)), ((), ())), preferred_element_type=f32)


def dot(a, b):
    return jnp.dot(a, b, preferred_element_type=f32)


class Link:
    def __init__(self, send_sem, recv_sem):
        self.ss, self.rs = send_sem, recv_sem
        self.me = {a: lax.axis_index(a) for a in SIZE}
        self.sent = []

    def peer(self, axis, step):
        return {axis: lax.rem(self.me[axis] + step + SIZE[axis], SIZE[axis])}

    def send(self, src, dst, axis, step):
        k = len(self.sent)
        copy = pltpu.make_async_remote_copy(
            src_ref=src,
            dst_ref=dst,
            send_sem=self.ss.at[k],
            recv_sem=self.rs.at[k],
            device_id=self.peer(axis, step),
            device_id_type=MESH,
        )
        copy.start()
        self.sent.append(copy)
        return copy


class Gather:
    def __init__(self, link, buf, plan):
        self.link, self.buf = link, buf
        self.waiting = []
        self.steps = []
        for first, (dim, form) in zip((True, False), plan):
            if form == "ring":
                for hop in range(1, SIZE[dim] // 2 + 1):
                    self.steps.append(functools.partial(self.ring, dim, first, hop))
            elif form == "direct":
                self.steps.append(functools.partial(self.direct, dim, first))
            else:
                self.steps.append(functools.partial(self.two, dim, first, 1))
                self.steps.append(functools.partial(self.two, dim, first, 2))
        self.steps.append(self.core)
        self.steps.append(self.arrive)

    def at(self, dim, first, step, part=None):
        me = self.link.me
        i = lax.rem(me[dim] + step + SIZE[dim], SIZE[dim])
        cols = self.buf.shape[-1]
        half = pl.ds(0 if part is None else part * (cols // 2), cols // 2)
        if dim == "z":
            if first:
                if part is None:
                    return self.buf.at[i, me["y"], me["c"]]
                return self.buf.at[i, me["y"], me["c"], :, half]
            if part is None:
                return self.buf.at[i, :, me["c"]]
            return self.buf.at[i, pl.ds(part * (NY // 2), NY // 2), me["c"]]
        if first:
            if part is None:
                return self.buf.at[me["z"], i, me["c"]]
            return self.buf.at[me["z"], i, me["c"], :, half]
        if part is None:
            return self.buf.at[:, i, me["c"]]
        return self.buf.at[pl.ds(part * (NZ // 2), NZ // 2), i, me["c"]]

    def send(self, view, axis, step):
        self.waiting.append(self.link.send(view, view, axis, step))

    def arrive(self):
        for copy in self.waiting:
            copy.wait_recv()
        self.waiting = []

    def ring(self, dim, first, hop):
        self.arrive()
        last = hop == SIZE[dim] // 2
        self.send(self.at(dim, first, 1 - hop, 0 if last else None), dim, 1)
        self.send(self.at(dim, first, hop - 1, 1 if last else None), dim, -1)

    def direct(self, dim, first):
        self.arrive()
        for step in range(1, SIZE[dim]):
            self.send(self.at(dim, first, 0), dim, step)

    def two(self, dim, first, hop):
        self.arrive()
        if hop == 1:
            for step in (1, -1, 2, -2):
                self.send(self.at(dim, first, 0), dim, step)
        else:
            self.send(self.at(dim, first, -2), dim, 1)
            self.send(self.at(dim, first, 2), dim, -1)
            if self.buf.shape[-1] < 256:
                self.send(self.at(dim, first, -2), dim, 2)
                return
            self.send(self.at(dim, first, -2, 0), dim, 2)
            self.send(self.at(dim, first, 2, 1), dim, -2)

    def core(self):
        self.arrive()
        self.send(self.buf.at[:, :, self.link.me["c"]], "c", 1)


def flat(ref):
    return ref[...].reshape(-1, ref.shape[-1])


def norm_rows(src, dst, gain, rows, block=16, unroll=4):
    start, count = rows

    def body(i, _):
        at = pl.ds(pl.multiple_of(start + i * block, block), block)
        v = src[at, :].astype(f32)
        scale = lax.rsqrt(jnp.mean(v * v, axis=-1, keepdims=True) + 1e-06)
        dst[at, :] = (v * scale * gain[...]).astype(bf16)
        return 0

    lax.fori_loop(0, count // block, body, 0, unroll=unroll)


PLANS = {
    "k": (("z", "two"), ("y", "direct")),
    "q0": (("z", "two"), ("y", "direct")),
    "q1": (("y", "direct"), ("z", "ring")),
    "v": (("y", "direct"), ("z", "ring")),
    "a": (("z", "two"), ("y", "direct")),
    "o": (("z", "two"), ("y", "direct")),
    "g": (("z", "ring"), ("y", "ring")),
    "u": (("y", "ring"), ("z", "ring")),
    "d": (("y", "ring"), ("z", "ring")),
}
ORDER = (
    "q1.0", "k.0", "a.0", "q0.0", "v.0", "h", "q1.1", "n0", "k.1", "a.1", "v.1", "q0.1", "n1",
    "u.0", "q1.2", "g.0", "d.0", "n2", "k.2", "a.2", "o.0", "n3", "v.2", "q0.2", "u.1", "d.1",
    "q1.3", "g.1", "o.1", "v.3", "q1.4", "g.2", "o.2", "k.3", "v.4", "q1.5", "a.3", "k.4", "pk0",
    "g.3", "pk1", "q1.6", "qb", "a.4", "kv", "q0.3", "v.5", "u.2", "pk2", "d.2", "g.4", "pk3",
    "q0.4", "qa", "v.6", "pv0", "pv1", "pv2", "pv3", "t0", "u.3", "o.3", "t1", "d.3", "t2", "t3",
    "u.4", "g.5", "d.4", "o.4", "omA", "omB", "u.5", "g.6", "d.5", "mnA", "u.6", "mnB", "d.6",
    "g.7", "u.7", "fA", "d.7", "dA", "fB", "dB", "eA", "eB",
)


def kernel(
    lens,
    tix,
    acts,
    noise,
    prefix,
    inv_period,
    prefix_gain,
    attn_gain,
    mlp_gain,
    final_gain,
    action_in,
    head_t,
    key_w,
    value_w,
    query_w,
    akey_w,
    avalue_w,
    out_t,
    gate_w,
    up_w,
    down_t,
    vel_ref,
    loss_ref,
    kb,
    vb,
    q0b,
    q1b,
    ab,
    ob,
    gb,
    ub,
    db,
    pre,
    pk,
    pv,
    ain,
    hdt,
    actv,
    noisev,
    h0,
    an,
    akvs,
    akv,
    qs,
    qall,
    ares,
    aall,
    part,
    part2,
    r1,
    r2,
    h1,
    mn,
    hid,
    fn,
    send_sem,
    recv_sem,
    local_sem,
):
    link = Link(send_sem, recv_sem)
    me = link.me
    z, y, c, x = (me[a] for a in DP_MP)
    span = acts.shape[2]
    count = [0]

    def fetch(src, dst):
        copy = pltpu.make_async_copy(src, dst, local_sem.at[count[0]])
        copy.start()
        count[0] += 1
        return copy

    barrier = pltpu.get_barrier_semaphore()
    near = [("z", s) for s in (1, -1, 2, -2)] + [("y", s) for s in (1, 2, 3)]
    near += [("c", 1)] + [("mp", s) for s in (1, 2, 3)]
    for axis, step in near:
        pl.semaphore_signal(barrier, inc=1, device_id=link.peer(axis, step), device_id_type=MESH)
    side = pl.ds(pl.multiple_of(lax.rem(x, 2) * 128, 128), 128)
    quarter_sem = local_sem.at[LOCALS - 1]
    action_block = pltpu.make_async_copy(akey_w.at[:, side], ab.at[z, y, c], quarter_sem)

    @pl.when(x < 2)
    def _():
        action_block.start()

    @pl.when(x >= 2)
    def _():
        pltpu.make_async_copy(avalue_w.at[:, side], ab.at[z, y, c], quarter_sem).start()

    early = [
        action_block,
        fetch(key_w, kb.at[z, y, c]),
        fetch(query_w.at[:, pl.ds(0, 256)], q0b.at[z, y, c]),
        fetch(query_w.at[:, pl.ds(256, 256)], q1b.at[z, y, c]),
        fetch(value_w, vb.at[z, y, c]),
    ]
    small = [
        fetch(action_in, ain),
        fetch(acts, actv),
        fetch(noise, noisev),
        fetch(head_t, hdt),
    ]
    late = {
        "o": fetch(out_t, ob.at[z, y, c]),
        "g": fetch(gate_w, gb.at[z, y, c]),
        "u": fetch(up_w, ub.at[z, y, c]),
        "d": fetch(down_t, db.at[z, y, c]),
    }
    quarter = prefix.shape[0] // 4
    chunks = [
        fetch(prefix.at[pl.ds(i * quarter, quarter)], pre.at[pl.ds(i * quarter, quarter)])
        for i in range(4)
    ]
    bufs = {
        "k": kb, "v": vb, "q0": q0b, "q1": q1b, "a": ab, "o": ob, "g": gb, "u": ub, "d": db,
    }
    gathers = {name: Gather(link, buf, PLANS[name]) for name, buf in bufs.items()}
    own = pl.ds(pl.multiple_of(x * PAD, PAD), PAD)
    flight = {}
    tasks = {}

    def task(fn, name, *args):
        tasks[name] = functools.partial(fn, *args)

    def others(src, dst, rows):
        at = pl.ds(*rows)
        return [
            link.send(src.at[lax.rem(x + step, NX), at], dst.at[step, at], "mp", step)
            for step in range(1, NX)
        ]

    def arrived(name):
        for copy in flight[name]:
            copy.wait_recv()

    def embed():
        for copy in small:
            copy.wait()
        for e in range(4):
            t = (tix[e].astype(f32) + 0.5) * (1.0 / TSTEPS)
            u = t * inv_period[...]
            turn = (u - jnp.floor(u + 0.5)) * (2.0 * math.pi)
            half = turn.shape[1]
            x_t = t * noisev[e] + (1.0 - t) * actv[e]
            mixed = lax.dot_general(
                x_t.astype(bf16), ain[...], (((0,), (0,)), ((), ())), preferred_element_type=f32
            )
            h0[(e + 1) * PAD - 16 : (e + 1) * PAD, :] = jnp.zeros((16, 2 * half), f32)
            at = pl.ds(e * PAD, span)
            h0[at, 0:half] = mixed[:, 0:half] + jnp.sin(turn)
            h0[at, half:] = mixed[:, half:] + jnp.cos(turn)
        norm_rows(h0, an, attn_gain, (0, 4 * PAD))

    task(embed, "h")

    def prefix_norm(i):
        chunks[i].wait()
        norm_rows(pre, pre, prefix_gain, (i * quarter, quarter))

    def project_query(h):
        q = (dot(an[...], flat((q0b, q1b)[h])) * 0.0625).astype(bf16)
        qs[h] = q.reshape(4, PAD, 256)
        at = pl.ds(0, ROWS)
        flight["q%d" % h] = [
            link.send(qs.at[h, lax.rem(x + step, NX), at], qall.at[x, h, at], "mp", step)
            for step in range(1, NX)
        ]
        qall[x, h] = qs[h, x]

    task(project_query, "qa", 0)
    task(project_query, "qb", 1)

    def project_action():
        akvs[...] = dot(an[...], flat(ab)).astype(bf16).reshape(4, PAD, 128)
        flight["kv"] = [
            link.send(akvs.at[lax.rem(x + step, NX)], akv.at[x], "mp", step)
            for step in range(1, NX)
        ]
        akv[x] = akvs[x]

    task(project_action, "kv")

    def project_prefix(i, weight, dst):
        at = pl.ds(i * quarter, quarter)
        dst[at, :] = dot(pre[at, :], flat(weight)).astype(bf16)

    for i in range(4):
        task(prefix_norm, "n%d" % i, i)
        task(project_prefix, "pk%d" % i, i, kb, pk)
        task(project_prefix, "pv%d" % i, i, vb, pv)

    def attend(step):
        if step == 0:
            arrived("kv")
            flight["r"] = []
        src = lax.rem(x - step + NX, NX)
        if step:
            for h in range(2):
                flight["q%d" % h][step - 1].wait_recv()
        rows = qall[src].reshape(2 * PAD, 256)
        s = nt(rows, pk[...])
        live = lax.broadcasted_iota(jnp.int32, s.shape, 1) < lens[x]
        p = jnp.where(live, jnp.exp(s), 0.0)
        sa = nt(rows, jnp.concatenate([akv[0], akv[1]], axis=1))
        real = lax.broadcasted_iota(jnp.int32, sa.shape, 1) < span
        pa = jnp.where(real, jnp.exp(sa), 0.0)
        total = jnp.sum(p, axis=-1, keepdims=True) + jnp.sum(pa, axis=-1, keepdims=True)
        mixed = dot(p.astype(bf16), pv[...])
        mixed = mixed + dot(pa.astype(bf16), jnp.concatenate([akv[2], akv[3]], axis=1))
        done = (mixed / total).astype(bf16).reshape(2, PAD, 256)
        if step:
            ares[step] = done
            at = pl.ds(0, ROWS)
            flight["r"].append(
                link.send(ares.at[step, :, at], aall.at[x, :, at], "mp", -step)
            )
        else:
            aall[x] = done

    for step in range(4):
        task(attend, "t%d" % step, step)

    def out_part(wave, start, rows):
        if wave == "A":
            arrived("r")
        at = slice(start, start + 32)
        a0 = aall[:, 0, at].reshape(128, 256)
        a1 = aall[:, 1, at].reshape(128, 256)
        w = flat(ob)
        for j in range(4):
            cols = slice(j * 256, (j + 1) * 256)
            value = nt(a0, w[cols, 0:256]) + nt(a1, w[cols, 256:512])
            part[:, at, cols] = value.astype(bf16).reshape(4, 32, 256)
        flight["p" + wave] = others(part, r1, (start, rows))

    def summed(base, mine, got, at):
        return (
            base
            + mine[x, at].astype(f32)
            + got[1, at].astype(f32)
            + got[2, at].astype(f32)
            + got[3, at].astype(f32)
        )

    def middle(wave, start, rows):
        arrived("p" + wave)
        at = slice(start, start + 32)
        mine = pl.ds(pl.multiple_of(x * PAD + start, 32), 32)
        h1[at, :] = summed(h0[mine, :], part, r1, at)
        norm_rows(h1, mn.at[x], mlp_gain, (start, 32), unroll=2)
        send = pl.ds(start, rows)
        flight["m" + wave] = [
            link.send(mn.at[x, send], mn.at[x, send], "mp", step) for step in range(1, NX)
        ]

    def feed(wave, start, rows):
        arrived("m" + wave)
        rows_in = mn[:, start : start + 32].reshape(128, -1)
        at = pl.ds(start * 4, 128)
        for j in range(4):
            cols = pl.ds(j * 256, 256)
            wg = gb[:, :, :, :, cols].reshape(-1, 256)
            wu = ub[:, :, :, :, cols].reshape(-1, 256)
            act = jax.nn.gelu(dot(rows_in, wg), approximate=True)
            hid[at, cols] = (act * dot(rows_in, wu)).astype(bf16)

    def down_part(wave, start, rows):
        at = slice(start, start + 32)
        value_in = hid[start * 4 : start * 4 + 128, :]
        w = flat(db)
        for j in range(4):
            cols = slice(j * 256, (j + 1) * 256)
            value = nt(value_in, w[cols]).astype(bf16)
            part2[:, at, cols] = value.reshape(4, 32, 256)
        flight["s" + wave] = others(part2, r2, (start, rows))

    def finish(wave, start, rows):
        arrived("s" + wave)
        at = slice(start, start + 32)
        h1[at, :] = summed(h1[at, :], part2, r2, at)
        norm_rows(h1, fn, final_gain, (start, 32), unroll=2)
        if wave == "B":
            velocity = nt(hdt[...], fn[...])[:, 0:span]
            vel_ref[0] = velocity
            diff = velocity - (noisev[x] - actv[x])
            square = jnp.sum(diff * diff, axis=0, keepdims=True)
            scale = 1.0 / (diff.shape[0] * diff.shape[1])
            loss_ref[...] = jnp.sum(square, axis=1, keepdims=True) * scale

    for wave in (("A", 0, 32), ("B", 32, ROWS - 32)):
        task(out_part, "om" + wave[0], *wave)
        task(middle, "mn" + wave[0], *wave)
        task(feed, "f" + wave[0], *wave)
        task(down_part, "d" + wave[0], *wave)
        task(finish, "e" + wave[0], *wave)

    for copy in early:
        copy.wait()
    pl.semaphore_wait(barrier, len(near))
    for name in ORDER:
        if "." not in name:
            tasks[name]()
            continue
        item, step = name.split(".")
        if step == "0" and item in late:
            late[item].wait()
        gathers[item].steps[int(step)]()
    for copy in link.sent:
        copy.wait_send()


def on_device(
    prefix_hidden,
    prefix_len,
    actions,
    noise,
    time_index,
    prefix_gain,
    key_weight,
    value_weight,
    action_in,
    attn_gain,
    query_w,
    akey_w,
    avalue_w,
    out_w,
    mlp_gain,
    gate_w,
    up_w,
    down_w,
    final_gain,
    head_w,
):
    positions, width = prefix_hidden.shape[1:]
    group_eps, span, adim = actions.shape
    expert = action_in.shape[1]
    half = expert // 2
    inv_period = (250.0 * 1000.0 ** (-np.arange(half) / (half - 1))).astype(np.float32)
    vmem = pl.BlockSpec(memory_space=pltpu.VMEM)
    smem = pl.BlockSpec(memory_space=pltpu.SMEM)
    hbm = pl.BlockSpec(memory_space=pltpu.HBM)
    operands = [
        (prefix_len, smem),
        (time_index, smem),
        (actions.transpose(0, 2, 1), hbm),
        (noise.transpose(0, 2, 1), hbm),
        (prefix_hidden.reshape(positions, width), hbm),
        (jnp.asarray(inv_period)[None, :], vmem),
        (prefix_gain[None, :], vmem),
        (attn_gain[None, :], vmem),
        (mlp_gain[None, :], vmem),
        (final_gain[None, :], vmem),
        (action_in, hbm),
        (head_w.T, hbm),
        (key_weight, hbm),
        (value_weight, hbm),
        (query_w, hbm),
        (akey_w, hbm),
        (avalue_w, hbm),
        (out_w.T, hbm),
        (gate_w, hbm),
        (up_w, hbm),
        (down_w.T, hbm),
    ]

    def weight(rows, cols):
        return pltpu.VMEM((NZ, NY, NC, rows, cols), bf16)

    rows = group_eps * PAD
    velocity, loss = pl.pallas_call(
        kernel,
        out_shape=(
            jax.ShapeDtypeStruct((1, adim, span), f32),
            jax.ShapeDtypeStruct((1, 1), f32),
        ),
        in_specs=[spec for _, spec in operands],
        out_specs=(vmem, vmem),
        scratch_shapes=[
            weight(32, 256),
            weight(32, 256),
            weight(16, 256),
            weight(16, 256),
            weight(16, 128),
            weight(16, 512),
            weight(16, 1024),
            weight(16, 1024),
            weight(16, 1024),
            pltpu.VMEM((positions, width), bf16),
            pltpu.VMEM((positions, 256), bf16),
            pltpu.VMEM((positions, 256), bf16),
            pltpu.VMEM((adim, expert), bf16),
            pltpu.VMEM((adim, expert), bf16),
            pltpu.VMEM((group_eps, adim, span), f32),
            pltpu.VMEM((group_eps, adim, span), f32),
            pltpu.VMEM((rows, expert), f32),
            pltpu.VMEM((rows, expert), bf16),
            pltpu.VMEM((NX, PAD, 128), bf16),
            pltpu.VMEM((NX, PAD, 128), bf16),
            pltpu.VMEM((2, NX, PAD, 256), bf16),
            pltpu.VMEM((NX, 2, PAD, 256), bf16),
            pltpu.VMEM((NX, 2, PAD, 256), bf16),
            pltpu.VMEM((NX, 2, PAD, 256), bf16),
            pltpu.VMEM((NX, PAD, expert), bf16),
            pltpu.VMEM((NX, PAD, expert), bf16),
            pltpu.VMEM((NX, PAD, expert), bf16),
            pltpu.VMEM((NX, PAD, expert), bf16),
            pltpu.VMEM((PAD, expert), f32),
            pltpu.VMEM((NX, PAD, expert), bf16),
            pltpu.VMEM((rows, 1024), bf16),
            pltpu.VMEM((PAD, expert), bf16),
            pltpu.SemaphoreType.DMA((SENDS,)),
            pltpu.SemaphoreType.DMA((SENDS,)),
            pltpu.SemaphoreType.DMA((LOCALS,)),
        ],
        compiler_params=pltpu.CompilerParams(
            collective_id=0, has_side_effects=True, vmem_limit_bytes=56 << 20
        ),
    )(*[value for value, _ in operands])
    return velocity.transpose(0, 2, 1), loss.reshape(1)


def solution(mesh):
    split = Mesh(mesh.devices.reshape(NZ, NY, NC, NX), DP_MP)
    placed = (
        P(DP_MP, None, None),
        P(DP),
        P(DP, None, None),
        P(DP, None, None),
        P(DP),
        P(),
        P(DP, None),
        P(DP, None),
        P(),
        P(),
        P(DP, "mp"),
        P(DP, None),
        P(DP, None),
        P("mp", DP),
        P(),
        P(DP, "mp"),
        P(DP, "mp"),
        P("mp", DP),
        P(),
        P(),
    )
    return jax.shard_map(
        on_device,
        mesh=split,
        in_specs=placed,
        out_specs=(P(DP_MP, None, None), P(DP_MP)),
        check_vma=False,
    )
```

time: 107 us -> 77 us (0.72)
  Pallas kernels: 100 us -> 73.1 us
  other arithmetic: 1.61 us -> 0 us
    pallas_call x1, Pallas kernels: 100 us -> 73.1 us  [on_device(): pl.pallas_call(kernel, out_shape=(jax.ShapeDtypeStruct((1, adim, span), f...]
where the time goes in v3:
time: 77 us; the launch traced here: 76.8 us
  Pallas kernels  73.1 us (95%)
  between operations  2.41 us (3%)
  local copies, waits for them, and re-layouts  1.32 us (2%)
    pallas_call x1, Pallas kernels, on_device(): pl.pallas_call(kernel, out_shape=(jax.ShapeDtypeStruct((1, adim, span), f...  73.1 us

profile of v3, /device:TPU:1, one launch (start us, length us, event | category | flops | bytes accessed | tf_op | source)
XLA Modules:
  0.0 76.8 jit_solution(2363660803779258484)
XLA Ops:
  0.6 73.1 %shard_map.212 = (f32[1,32,50]{2,1,0:T(8,128)}, f32[1,1]{1,0:T(1,128)}) custom-call(s32[4]{0:T(128)} %lens.1, s32[4]{0:T(128)} %tix.1, f32[4,32,50]{2,1,0:T(8,128)} %bitcast.13, f32[4,32,50]{2,1,0:T(8,128)} %bitcast.14, bf16[1024,2048]{1,0:T(8,128)(2,1)} %bitcast.12, f32[1,512]{1,0:T(1,128)} %constant.17.inv_period, f32[1,2048]{1,0:T(1,128)} %bitcast.19, ...), custom_call_target="tpu_custom_call" | custom-call | tf_op jit(solution)/shard_map/pallas_call | solution.py:542
  73.7 1.3 %copy.25 = f32[1,50,32]{1,2,0:T(8,128)} copy(f32[1,50,32]{1,2,0:T(8,128)} %bitcast.18) | data formatting | bytes 12800

commit v4 on v3

--- a/solution.py
+++ b/solution.py
@@ -149,24 +149,24 @@
 
 
 PLANS = {
-    "k": (("z", "two"), ("y", "direct")),
-    "q0": (("z", "two"), ("y", "direct")),
-    "q1": (("y", "direct"), ("z", "ring")),
+    "k": (("z", "two"), ("y", "ring")),
+    "q0": (("z", "two"), ("y", "ring")),
+    "q1": (("z", "two"), ("y", "ring")),
     "v": (("y", "direct"), ("z", "ring")),
     "a": (("z", "two"), ("y", "direct")),
-    "o": (("z", "two"), ("y", "direct")),
-    "g": (("z", "ring"), ("y", "ring")),
+    "o": (("z", "ring"), ("y", "ring")),
+    "g": (("z", "two"), ("y", "ring")),
     "u": (("y", "ring"), ("z", "ring")),
-    "d": (("y", "ring"), ("z", "ring")),
+    "d": (("z", "two"), ("y", "ring")),
 }
 ORDER = (
-    "q1.0", "k.0", "a.0", "q0.0", "v.0", "h", "q1.1", "n0", "k.1", "a.1", "v.1", "q0.1", "n1",
-    "u.0", "q1.2", "g.0", "d.0", "n2", "k.2", "a.2", "o.0", "n3", "v.2", "q0.2", "u.1", "d.1",
-    "q1.3", "g.1", "o.1", "v.3", "q1.4", "g.2", "o.2", "k.3", "v.4", "q1.5", "a.3", "k.4", "pk0",
-    "g.3", "pk1", "q1.6", "qb", "a.4", "kv", "q0.3", "v.5", "u.2", "pk2", "d.2", "g.4", "pk3",
-    "q0.4", "qa", "v.6", "pv0", "pv1", "pv2", "pv3", "t0", "u.3", "o.3", "t1", "d.3", "t2", "t3",
-    "u.4", "g.5", "d.4", "o.4", "omA", "omB", "u.5", "g.6", "d.5", "mnA", "u.6", "mnB", "d.6",
-    "g.7", "u.7", "fA", "d.7", "dA", "fB", "dB", "eA", "eB",
+    "q0.0", "v.0", "k.0", "o.0", "q1.0", "h", "n0", "q0.1", "v.1", "n1", "n2", "k.1", "o.1",
+    "q1.1", "n3", "q0.2", "a.0", "u.0", "v.2", "k.2", "o.2", "q1.2", "g.0", "a.1", "q0.3", "u.1",
+    "v.3", "o.3", "d.0", "k.3", "g.1", "a.2", "q1.3", "q0.4", "v.4", "o.4", "u.2", "q0.5", "qa",
+    "k.4", "d.1", "a.3", "g.2", "q1.4", "k.5", "pk0", "v.5", "pk1", "a.4", "kv", "q1.5", "qb",
+    "pk2", "pk3", "v.6", "pv0", "o.5", "u.3", "pv1", "pv2", "pv3", "t0", "d.2", "t1", "t2", "t3",
+    "g.3", "u.4", "o.6", "o.7", "omA", "omB", "u.5", "d.3", "g.4", "mnA", "u.6", "mnB", "d.4",
+    "g.5", "u.7", "fA", "d.5", "dA", "fB", "dB", "eA", "eB",
 )
 
 

time: 77 us -> 73.8 us (0.958); the launches traced: 76.8 us -> 72.6 us
  Pallas kernels: 73.1 us -> 68.9 us
    pallas_call x1, Pallas kernels: 73.1 us -> 68.9 us  [on_device(): pl.pallas_call(kernel, out_shape=(jax.ShapeDtypeStruct((1, adim, span), f...]
where the time goes in v4:
time: 73.8 us; the launch traced here: 72.6 us
  Pallas kernels  68.9 us (93%)
  between operations  2.41 us (3%)
  local copies, waits for them, and re-layouts  1.32 us (2%)
    pallas_call x1, Pallas kernels, on_device(): pl.pallas_call(kernel, out_shape=(jax.ShapeDtypeStruct((1, adim, span), f...  68.9 us

profile of v4, /device:TPU:1, one launch (start us, length us, event | category | flops | bytes accessed | tf_op | source)
XLA Modules:
  0.0 72.6 jit_solution(6286720842343549443)
XLA Ops:
  0.6 68.9 %shard_map.212 = (f32[1,32,50]{2,1,0:T(8,128)}, f32[1,1]{1,0:T(1,128)}) custom-call(s32[4]{0:T(128)} %lens.1, s32[4]{0:T(128)} %tix.1, f32[4,32,50]{2,1,0:T(8,128)} %bitcast.13, f32[4,32,50]{2,1,0:T(8,128)} %bitcast.14, bf16[1024,2048]{1,0:T(8,128)(2,1)} %bitcast.12, f32[1,512]{1,0:T(1,128)} %constant.17.inv_period, f32[1,2048]{1,0:T(1,128)} %bitcast.19, ...), custom_call_target="tpu_custom_call" | custom-call | tf_op jit(solution)/shard_map/pallas_call | solution.py:542
  69.5 1.3 %copy.25 = f32[1,50,32]{1,2,0:T(8,128)} copy(f32[1,50,32]{1,2,0:T(8,128)} %bitcast.18) | data formatting | bytes 12800

commit v5 on v3

--- a/solution.py
+++ b/solution.py
@@ -154,19 +154,19 @@
     "q1": (("y", "direct"), ("z", "ring")),
     "v": (("y", "direct"), ("z", "ring")),
     "a": (("z", "two"), ("y", "direct")),
-    "o": (("z", "two"), ("y", "direct")),
+    "o": (("z", "two"), ("y", "ring")),
     "g": (("z", "ring"), ("y", "ring")),
     "u": (("y", "ring"), ("z", "ring")),
     "d": (("y", "ring"), ("z", "ring")),
 }
 ORDER = (
-    "q1.0", "k.0", "a.0", "q0.0", "v.0", "h", "q1.1", "n0", "k.1", "a.1", "v.1", "q0.1", "n1",
-    "u.0", "q1.2", "g.0", "d.0", "n2", "k.2", "a.2", "o.0", "n3", "v.2", "q0.2", "u.1", "d.1",
-    "q1.3", "g.1", "o.1", "v.3", "q1.4", "g.2", "o.2", "k.3", "v.4", "q1.5", "a.3", "k.4", "pk0",
-    "g.3", "pk1", "q1.6", "qb", "a.4", "kv", "q0.3", "v.5", "u.2", "pk2", "d.2", "g.4", "pk3",
-    "q0.4", "qa", "v.6", "pv0", "pv1", "pv2", "pv3", "t0", "u.3", "o.3", "t1", "d.3", "t2", "t3",
-    "u.4", "g.5", "d.4", "o.4", "omA", "omB", "u.5", "g.6", "d.5", "mnA", "u.6", "mnB", "d.6",
-    "g.7", "u.7", "fA", "d.7", "dA", "fB", "dB", "eA", "eB",
+    "q1.0", "q0.0", "v.0", "a.0", "k.0", "g.0", "q1.1", "h", "q0.1", "v.1", "a.1", "u.0", "d.0",
+    "k.1", "q1.2", "g.1", "q0.2", "o.0", "v.2", "a.2", "u.1", "k.2", "q1.3", "d.1", "g.2", "n0",
+    "n1", "o.1", "q0.3", "v.3", "n2", "q1.4", "a.3", "u.2", "g.3", "n3", "q0.4", "qa", "o.2",
+    "a.4", "kv", "v.4", "q1.5", "q1.6", "qb", "k.3", "d.2", "u.3", "g.4", "v.5", "k.4", "pk0",
+    "pk1", "pk2", "pk3", "o.3", "v.6", "pv0", "pv1", "pv2", "pv3", "t0", "t1", "d.3", "t2", "t3",
+    "u.4", "g.5", "o.4", "d.4", "o.5", "omA", "omB", "u.5", "g.6", "d.5", "mnA", "u.6", "mnB",
+    "d.6", "g.7", "u.7", "fA", "d.7", "dA", "fB", "dB", "eA", "eB",
 )
 
 

time: 77 us -> 72.7 us (0.944)
  Pallas kernels: 73.1 us -> 68.7 us
    pallas_call x1, Pallas kernels: 73.1 us -> 68.7 us  [on_device(): pl.pallas_call(kernel, out_shape=(jax.ShapeDtypeStruct((1, adim, span), f...]
where the time goes in v5:
time: 72.7 us; the launch traced here: 72.5 us
  Pallas kernels  68.7 us (94%)
  between operations  2.41 us (3%)
  local copies, waits for them, and re-layouts  1.32 us (2%)
    pallas_call x1, Pallas kernels, on_device(): pl.pallas_call(kernel, out_shape=(jax.ShapeDtypeStruct((1, adim, span), f...  68.7 us

profile of v5, /device:TPU:1, one launch (start us, length us, event | category | flops | bytes accessed | tf_op | source)
XLA Modules:
  0.0 72.5 jit_solution(2291805385220991594)
XLA Ops:
  0.6 68.7 %shard_map.212 = (f32[1,32,50]{2,1,0:T(8,128)}, f32[1,1]{1,0:T(1,128)}) custom-call(s32[4]{0:T(128)} %lens.1, s32[4]{0:T(128)} %tix.1, f32[4,32,50]{2,1,0:T(8,128)} %bitcast.13, f32[4,32,50]{2,1,0:T(8,128)} %bitcast.14, bf16[1024,2048]{1,0:T(8,128)(2,1)} %bitcast.12, f32[1,512]{1,0:T(1,128)} %constant.17.inv_period, f32[1,2048]{1,0:T(1,128)} %bitcast.19, ...), custom_call_target="tpu_custom_call" | custom-call | tf_op jit(solution)/shard_map/pallas_call | solution.py:542
  69.4 1.3 %copy.25 = f32[1,50,32]{1,2,0:T(8,128)} copy(f32[1,50,32]{1,2,0:T(8,128)} %bitcast.18) | data formatting | bytes 12800
